TPU v7x, 256 devices: a whole 4x4x8 slice. The times are simulated.
256 devices in a mesh: seq: 32 (over y, z), ch: 8 (over x, core).
Axes of the slice: x: 4, y: 4, z: 8, core: 2. Of those that a mesh axis runs over, the one named last changes fastest.
Arguments:
- genome: int32 [8192, 128], P('seq'), may hold values from 0 to 3
- stem_weight: bfloat16 [768, 512], P('ch'), may hold values from -0.5 to 0.5
- dilated_filter_weight: bfloat16 [5, 3, 768, 768], P(None, None, 'ch'), may hold values from -0.125 to 0.125
- head_weight: bfloat16 [768, 5313], P('ch'), may hold values from -0.21875 to 0.21875
- window_start: int32 [512], replicated, may hold values from 0 to 8176
- window_track: int32 [512], replicated, may hold values from 0 to 5312
- targets: float32 [512], replicated, may hold values from 0 to 3
Outputs:
- window_score: float32 [512], replicated
- conv_grad: float32 [5, 3, 768, 768], P(None, None, 'ch', 'seq')
- stem_grad: float32 [768, 512], P('ch')
- head_grad: float32 [768, 5313], P('ch')
Inputs may be any that keep to these rules, and one draw needn't show every extreme that they name: `window_start`: each window lies inside the sequence.
All inputs are finite; a program needn't handle non-finite values.
Results may differ from a plain program's by a relative error of at most 0.0037.
Values may be sent and summed in bfloat16 or wider, within the bound.
A program may use at most 128 MiB of HBM per device.

v0:
```python
import jax
import jax.numpy as jnp
from jax import lax
from jax.sharding import PartitionSpec as P

LAYERS = 5
WIN = 16


def extended(block, sides, width):
    for axis, dim in sides:
        count = lax.axis_size(axis)
        forward = [(i, i + 1) for i in range(count - 1)]
        backward = [(target, source) for source, target in forward]
        low = lax.ppermute(
            lax.slice_in_dim(block, block.shape[dim] - width, None, axis=dim), axis, forward
        )
        high = lax.ppermute(lax.slice_in_dim(block, 0, width, axis=dim), axis, backward)
        block = jnp.concatenate([low, block, high], axis=dim)
    return block


def passed_along(value, axis, by):
    count = lax.axis_size(axis)
    pairs = [(i, i + by) for i in range(count) if 0 <= i + by < count]
    return lax.ppermute(value, axis, pairs)


def dilations(shard_rows):
    return (shard_rows // 8, shard_rows // 2, shard_rows, 2 * shard_rows, 4 * shard_rows)


def reach_rows(field, distance):
    shard_rows = field.shape[2]
    if distance < shard_rows:
        padded = extended(field, (("seq", 2),), distance)
        return (padded[:, :, :shard_rows], padded[:, :, 2 * distance :])
    hop_count = distance // shard_rows
    lower_rows = passed_along(field, "seq", hop_count)
    upper_rows = passed_along(field, "seq", -hop_count)
    return (lower_rows, upper_rows)


def order_taps(lower_rows, middle, upper_rows):
    forward_taps = jnp.stack([lower_rows[0], middle[0], upper_rows[0]])
    reverse_taps = jnp.stack([upper_rows[1], middle[1], lower_rows[1]])
    return jnp.stack([forward_taps, reverse_taps])


def shards(
    genome, stem_weight, dilated_filter_weight, head_weight, window_start, window_track, targets
):
    shard_rows = genome.shape[0]
    spans = dilations(shard_rows)
    letters = (
        (genome[:, :, None] == jnp.arange(4, dtype=jnp.int32))
        .astype(jnp.bfloat16)
        .reshape(shard_rows, -1)
    )
    strands = jnp.stack([letters, letters[:, ::-1]])
    residual_state = jnp.einsum(
        "sri,ci->scr", strands, stem_weight, preferred_element_type=jnp.float32
    )
    saved_states = []
    stored_taps = []
    for current_layer_index in range(LAYERS):
        active = jax.nn.gelu(residual_state).astype(jnp.bfloat16)
        lower_rows, upper_rows = reach_rows(active, spans[current_layer_index])
        resident_taps = order_taps(lower_rows, active, upper_rows)
        collected_taps = lax.all_gather(resident_taps, "ch", axis=2, tiled=True)
        saved_states.append(residual_state)
        stored_taps.append(collected_taps)
        residual_state = residual_state + jnp.einsum(
            "nezp,efz->nfp",
            collected_taps,
            dilated_filter_weight[current_layer_index],
            preferred_element_type=jnp.float32,
        )
    strand_total = residual_state[0] + residual_state[1]
    first_bin = lax.axis_index("seq") * shard_rows
    positions = first_bin + jnp.arange(shard_rows, dtype=jnp.int32)
    member = (
        (positions[None, :] >= window_start[:, None])
        & (positions[None, :] < window_start[:, None] + WIN)
    ).astype(jnp.float32)
    pooled = jnp.einsum("cr,kr->ck", strand_total, member, precision=lax.Precision.HIGHEST) / WIN
    columns = jnp.take(head_weight, window_track, axis=1).astype(jnp.float32)
    partial_score = 0.5 * jnp.sum(pooled * columns, axis=0)
    window_score = lax.psum(partial_score, ("seq", "ch"))
    counts = jnp.sum((window_track[:, None] == window_track[None, :]).astype(jnp.float32), axis=1)
    loss_slope = (jnp.exp(window_score) - targets) / counts
    window_terms = 0.5 * loss_slope[None, :] * pooled
    weights_back = 0.5 / WIN * loss_slope[None, :] * columns
    back_total = jnp.einsum("ck,kr->cr", weights_back, member, precision=lax.Precision.HIGHEST)
    grad_state = jnp.stack([back_total, back_total])
    layer_gradient_list = []
    for current_layer_index in reversed(range(LAYERS)):
        incoming_gradient = grad_state.astype(jnp.bfloat16)
        weight_part = jnp.einsum(
            "pygj,pij->yig",
            stored_taps[current_layer_index],
            incoming_gradient,
            preferred_element_type=jnp.float32,
        )
        layer_gradient_list.append(
            lax.psum_scatter(weight_part, "seq", scatter_dimension=2, tiled=True)
        )
        lower_rows, upper_rows = reach_rows(incoming_gradient, spans[current_layer_index])
        back_taps = order_taps(upper_rows, incoming_gradient, lower_rows)
        spread = jnp.einsum(
            "skor,koc->scr",
            back_taps,
            dilated_filter_weight[current_layer_index],
            preferred_element_type=jnp.float32,
        )
        through = lax.psum_scatter(spread, "ch", scatter_dimension=1, tiled=True)
        pullback = jax.vjp(jax.nn.gelu, saved_states[current_layer_index])[1]
        grad_state = grad_state + pullback(through)[0]
    conv_grad = jnp.stack(layer_gradient_list[::-1])
    stem_part = jnp.einsum(
        "sri,scr->ci", strands, grad_state.astype(jnp.bfloat16), preferred_element_type=jnp.float32
    )
    head_part = jnp.zeros(head_weight.shape, jnp.float32).at[:, window_track].add(window_terms)
    head_grad, stem_grad = lax.psum((head_part, stem_part), "seq")
    return (window_score, conv_grad, stem_grad, head_grad)


def solution(mesh):
    return jax.shard_map(
        shards,
        mesh=mesh,
        in_specs=(
            P("seq", None),
            P("ch", None),
            P(None, None, "ch", None),
            P("ch", None),
            P(),
            P(),
            P(),
        ),
        out_specs=(P(), P(None, None, "ch", "seq"), P("ch", None), P("ch", None)),
        check_vma=False,
    )
```

profile of v0, /device:TPU:1, one launch (start us, length us, event | category | flops | bytes accessed | tf_op | source)
XLA Modules:
  0.0 820.2 jit_solution(104383886669573757)
XLA Ops:
  10.7 4.5 collective-permute-start
  16.5 3.7 collective-permute-done.1
  21.2 32.7 %all-gather.6.cloned.1.call-done = bf16[2,3,768,256]{3,2,1,0:T(8,128)(2,1)} async-done(((bf16[2,3,96,256]{3,2,1,0:T(8,128)(2,1)}), bf16[2,3,768,256]{3,2,1,0:T(8,128)(2,1)}) %all-gather.6.cloned.1.call-update) | async-done | bytes 2359312 | tf_op jit(solution)/shard_map/all_gather | solution.py:70
  56.1 3.2 collective-permute-start.2
  60.7 3.5 collective-permute-done.3
  65.0 30.5 %all-gather.8.cloned.1.call-done = bf16[2,3,768,256]{3,2,1,0:T(8,128)(2,1)} async-done(((bf16[2,3,96,256]{3,2,1,0:T(8,128)(2,1)}), bf16[2,3,768,256]{3,2,1,0:T(8,128)(2,1)}) %all-gather.8.cloned.1.call-update) | async-done | bytes 2359312 | tf_op jit(solution)/shard_map/all_gather | solution.py:70
  97.7 3.2 collective-permute-start.4
  102.8 3.8 collective-permute-done.5
  107.5 30.2 %all-gather.10.cloned.1.call-done = bf16[2,3,768,256]{3,2,1,0:T(8,128)(2,1)} async-done(((bf16[2,3,96,256]{3,2,1,0:T(8,128)(2,1)}), bf16[2,3,768,256]{3,2,1,0:T(8,128)(2,1)}) %all-gather.10.cloned.1.call-update) | async-done | bytes 2359312 | tf_op jit(solution)/shard_map/all_gather | solution.py:70
  139.9 4.2 collective-permute-start.6
  145.9 8.8 %collective-permute-done.7 = bf16[2,96,256]{2,1,0:T(8,128)(2,1)S(1)} collective-permute-done((bf16[2,96,256]{2,1,0:T(8,128)(2,1)S(1)}, bf16[2,96,256]{2,1,0:T(8,128)(2,1)S(1)}, u32[]{:S(2)}, u32[]{:S(2)}) %collective-permute-start.7) | collective-permute-done | bytes 98336 | tf_op jit(solution)/shard_map/ppermute | solution.py:26
  155.6 27.2 %all-gather.12.cloned.1.call-done = bf16[2,3,768,256]{3,2,1,0:T(8,128)(2,1)} async-done(((bf16[2,3,96,256]{3,2,1,0:T(8,128)(2,1)}), bf16[2,3,768,256]{3,2,1,0:T(8,128)(2,1)}) %all-gather.12.cloned.1.call-update) | async-done | bytes 2359312 | tf_op jit(solution)/shard_map/all_gather | solution.py:70
  185.0 7.4 collective-permute-start.8
  194.2 8.6 %collective-permute-done.9 = bf16[2,96,256]{2,1,0:T(8,128)(2,1)S(1)} collective-permute-done((bf16[2,96,256]{2,1,0:T(8,128)(2,1)S(1)}, bf16[2,96,256]{2,1,0:T(8,128)(2,1)S(1)}, u32[]{:S(2)}, u32[]{:S(2)}) %collective-permute-start.9) | collective-permute-done | bytes 98336 | tf_op jit(solution)/shard_map/ppermute | solution.py:26
  209.1 22.5 %all-gather.14.cloned.1.call-done = bf16[2,3,768,256]{3,2,1,0:T(8,128)(2,1)} async-done(((bf16[2,3,96,256]{3,2,1,0:T(8,128)(2,1)}), bf16[2,3,768,256]{3,2,1,0:T(8,128)(2,1)}) %all-gather.14.cloned.1.call-update) | async-done | bytes 2359312 | tf_op jit(solution)/shard_map/all_gather | solution.py:70
  235.0 76.7 %psum.21 = f32[512]{0:T(512)S(1)} all-reduce(f32[512]{0:T(512)S(1)} %broadcast_multiply_fusion), channel_id=1, replica_groups=mesh['seq'=32,'ch'=8] {'seq','ch'}, use_global_device_ids=true, to_apply=%region_1.2 | all-reduce | flops 512 | bytes 4096 | tf_op jit(solution)/shard_map/psum | solution.py:89
  313.5 7.9 collective-permute-start.11
  321.6 4.9 collective-permute-done.11
  328.3 32.8 %reduce-scatter.6.cloned.1.call-done = f32[2,96,256]{2,1,0:T(8,128)} async-done(((f32[2,768,256]{2,1,0:T(8,128)}), f32[2,96,256]{2,1,0:T(8,128)}) %reduce-scatter.6.cloned.1.call-update) | async-done | bytes 196624 | tf_op jit(solution)/shard_map/reduce_scatter | solution.py:116
  363.6 4.9 collective-permute-start.13
  372.0 39.8 %reduce-scatter.8.cloned.1.call-done = f32[2,96,256]{2,1,0:T(8,128)} async-done(((f32[2,768,256]{2,1,0:T(8,128)}), f32[2,96,256]{2,1,0:T(8,128)}) %reduce-scatter.8.cloned.1.call-update) | async-done | bytes 196624 | tf_op jit(solution)/shard_map/reduce_scatter | solution.py:116
  414.2 4.0 collective-permute-start.15
  421.7 37.6 %reduce-scatter.10.cloned.1.call-done = f32[2,96,256]{2,1,0:T(8,128)} async-done(((f32[2,768,256]{2,1,0:T(8,128)}), f32[2,96,256]{2,1,0:T(8,128)}) %reduce-scatter.10.cloned.1.call-update) | async-done | bytes 196624 | tf_op jit(solution)/shard_map/reduce_scatter | solution.py:116
  461.7 4.0 collective-permute-start.17
  468.7 37.7 %reduce-scatter.12.cloned.1.call-done = f32[2,96,256]{2,1,0:T(8,128)} async-done(((f32[2,768,256]{2,1,0:T(8,128)}), f32[2,96,256]{2,1,0:T(8,128)}) %reduce-scatter.12.cloned.1.call-update) | async-done | bytes 196624 | tf_op jit(solution)/shard_map/reduce_scatter | solution.py:116
  509.5 4.2 collective-permute-start.19
  514.8 2.9 convolution_bitcast_fusion
  521.2 4.4 scatter_custom_fusion
  532.1 2.7 convolution_bitcast_fusion.8
  538.7 16.7 %reduce-scatter.14.cloned.1.call-done = f32[2,96,256]{2,1,0:T(8,128)} async-done(((f32[2,768,256]{2,1,0:T(8,128)}), f32[2,96,256]{2,1,0:T(8,128)}) %reduce-scatter.14.cloned.1.call-update) | async-done | bytes 196624 | tf_op jit(solution)/shard_map/reduce_scatter | solution.py:116
  559.3 246.3 %all-reduce.8.cloned.1.call-done = (f32[3,96,768]{1,0,2:T(4,128)}, f32[3,96,768]{1,0,2:T(4,128)}, f32[3,96,768]{1,0,2:T(4,128)}, f32[3,96,768]{1,0,2:T(4,128)}, ...) async-done(((f32[3,96,768]{1,0,2:T(4,128)}, f32[3,96,768]{1,0,2:T(4,128)}, f32[3,96,768]{1,0,2:T(4,128)}, f32[3,96,768]{1,0,2:T(4,128)}, ...) | async-done | bytes 6660496
  805.6 3.2 copy.97
  (205 shorter events, 80.3 us)
Async XLA Ops:
  7.2 46.7 %all-gather.6.cloned.1.call-start = ((), (), s32[]{:S(2)}) async-start(), calls=%async_computation.5 | async-start | bytes 2654208 | tf_op jit(solution)/shard_map/all_gather | solution.py:70
  10.7 5.8 collective-permute-start
  15.2 5.0 collective-permute-start.1
  21.1 74.3 %all-gather.8.cloned.1.call-start = ((), (), s32[]{:S(2)}) async-start(), calls=%async_computation.6 | async-start | bytes 2654208 | tf_op jit(solution)/shard_map/all_gather | solution.py:70
  56.1 4.5 collective-permute-start.2
  59.3 4.8 collective-permute-start.3
  65.0 72.7 %all-gather.10.cloned.1.call-start = ((), (), s32[]{:S(2)}) async-start(), calls=%async_computation.7 | async-start | bytes 2654208 | tf_op jit(solution)/shard_map/all_gather | solution.py:70
  97.7 5.0 collective-permute-start.4
  100.9 5.7 collective-permute-start.5
  107.4 75.4 %all-gather.12.cloned.1.call-start = ((), (), s32[]{:S(2)}) async-start(), calls=%async_computation.8 | async-start | bytes 2654208 | tf_op jit(solution)/shard_map/all_gather | solution.py:70
  139.9 6.0 collective-permute-start.6
  144.0 10.6 %collective-permute-start.7 = (bf16[2,96,256]{2,1,0:T(8,128)(2,1)S(1)}, bf16[2,96,256]{2,1,0:T(8,128)(2,1)S(1)}, u32[]{:S(2)}, u32[]{:S(2)}) collective-permute-start(bf16[2,96,256]{2,1,0:T(8,128)(2,1)S(1)} %get-tuple-element.101), channel_id=1, source_target_pairs={{16,0},{24,8},{32,16},{40,24},{48,32},{56,40},{64,48},{72,56},{80,... | collective-permute-start | bytes 294920 | tf_op jit(solution)/shard_map/ppermute | solution.py:26
  155.5 76.1 %all-gather.14.cloned.1.call-start = ((), (), s32[]{:S(2)}) async-start(), calls=%async_computation.9 | async-start | bytes 2654208 | tf_op jit(solution)/shard_map/all_gather | solution.py:70
  185.0 9.1 %collective-permute-start.8 = (bf16[2,96,256]{2,1,0:T(8,128)(2,1)S(1)}, bf16[2,96,256]{2,1,0:T(8,128)(2,1)S(1)}, u32[]{:S(2)}, u32[]{:S(2)}) collective-permute-start(bf16[2,96,256]{2,1,0:T(8,128)(2,1)S(1)} %get-tuple-element.103), channel_id=1, source_target_pairs={{0,32},{8,40},{16,48},{24,56},{32,64},{40,72},{48,80},{56,88},{64,... | collective-permute-start | bytes 294920 | tf_op jit(solution)/shard_map/ppermute | solution.py:26
  192.4 10.3 %collective-permute-start.9 = (bf16[2,96,256]{2,1,0:T(8,128)(2,1)S(1)}, bf16[2,96,256]{2,1,0:T(8,128)(2,1)S(1)}, u32[]{:S(2)}, u32[]{:S(2)}) collective-permute-start(bf16[2,96,256]{2,1,0:T(8,128)(2,1)S(1)} %get-tuple-element.103), channel_id=1, source_target_pairs={{32,0},{40,8},{48,16},{56,24},{64,32},{72,40},{80,48},{88,56},{96,... | collective-permute-start | bytes 294920 | tf_op jit(solution)/shard_map/ppermute | solution.py:26
  203.6 157.6 %reduce-scatter.6.cloned.1.call-start = ((), (), s32[]{:S(2)}) async-start(), calls=%async_computation.10 | async-start | bytes 1769472 | tf_op jit(solution)/shard_map/reduce_scatter | solution.py:116
  208.7 103.0 %copy-start.23 = (f32[512]{0:T(512)S(1)}, f32[512]{0:T(512)}, u32[]{:S(2)}) copy-start(f32[512]{0:T(512)} %param.13) | copy-start | bytes 6148
  312.2 9.4 %collective-permute-start.10 = (bf16[2,96,256]{2,1,0:T(8,128)(2,1)S(1)}, bf16[2,96,256]{2,1,0:T(8,128)(2,1)S(1)}, u32[]{:S(2)}, u32[]{:S(2)}) collective-permute-start(bf16[2,96,256]{2,1,0:T(8,128)(2,1)S(1)} %fusion.101), channel_id=1, source_target_pairs={{32,0},{40,8},{48,16},{56,24},{64,32},{72,40},{80,48},{88,56},{96,... | collective-permute-start | bytes 294920 | tf_op jit(solution)/shard_map/ppermute | solution.py:26
  313.5 13.0 %collective-permute-start.11 = (bf16[2,96,256]{2,1,0:T(8,128)(2,1)S(1)}, bf16[2,96,256]{2,1,0:T(8,128)(2,1)S(1)}, u32[]{:S(2)}, u32[]{:S(2)}) collective-permute-start(bf16[2,96,256]{2,1,0:T(8,128)(2,1)S(1)} %fusion.101), channel_id=1, source_target_pairs={{0,32},{8,40},{16,48},{24,56},{32,64},{40,72},{48,80},{56,88},{64,... | collective-permute-start | bytes 294920 | tf_op jit(solution)/shard_map/ppermute | solution.py:26
  328.3 83.5 %reduce-scatter.8.cloned.1.call-start = ((), (), s32[]{:S(2)}) async-start(), calls=%async_computation.11 | async-start | bytes 1769472 | tf_op jit(solution)/shard_map/reduce_scatter | solution.py:116
  362.3 7.3 collective-permute-start.12
  363.6 6.5 collective-permute-start.13
  371.9 87.4 %reduce-scatter.10.cloned.1.call-start = ((), (), s32[]{:S(2)}) async-start(), calls=%async_computation.12 | async-start | bytes 1769472 | tf_op jit(solution)/shard_map/reduce_scatter | solution.py:116
  412.9 5.4 collective-permute-start.14
  414.2 5.6 collective-permute-start.15
  421.7 84.7 %reduce-scatter.12.cloned.1.call-start = ((), (), s32[]{:S(2)}) async-start(), calls=%async_computation.13 | async-start | bytes 1769472 | tf_op jit(solution)/shard_map/reduce_scatter | solution.py:116
  460.4 5.3 collective-permute-start.16
  461.7 5.2 collective-permute-start.17
  468.7 86.8 %reduce-scatter.14.cloned.1.call-start = ((), (), s32[]{:S(2)}) async-start(), calls=%async_computation.14 | async-start | bytes 1769472 | tf_op jit(solution)/shard_map/reduce_scatter | solution.py:116
  508.2 5.5 collective-permute-start.18
  509.5 5.2 collective-permute-start.19
  517.8 287.8 %all-reduce.8.cloned.1.call-start = ((), (), s32[]{:S(2)}) async-start(), calls=%async_computation.15 | async-start | bytes 21569536
  (24 other events, 288.8 us)
Sparse Core Ops, SparseCore 0:
  21.3 32.5 all-gather.5
  65.1 30.3 all-gather.7
  107.5 30.0 all-gather.9
  155.6 27.1 all-gather.11
  203.7 27.8 all-gather.13
  328.4 32.7 reduce-scatter.5
  372.0 39.7 reduce-scatter.7
  421.8 37.4 reduce-scatter.9
  468.8 37.5 reduce-scatter.11
  517.9 37.4 reduce-scatter.13
  560.7 244.8 all-reduce.7
where the time goes:
time: 822 us; the launch traced here: 820 us
  waiting for transfers between devices  594 us (72%)
  blocking collectives  76.7 us (9%)
  starting transfers between devices  60.7 us (7%)
  matrix products  32.7 us (4%)
  local copies, waits for them, and re-layouts  26.2 us (3%)
  between operations  15.4 us (2%)
  other arithmetic  14 us (2%)
    unnamed x12, waiting for transfers between devices  247 us
    reduce_scatter x5, waiting for transfers between devices, shards(): through = lax.psum_scatter(spread, 'ch', scatter_dimension=1, tiled=True)  165 us
    all_gather x5, waiting for transfers between devices, shards(): collected_taps = lax.all_gather(resident_taps, 'ch', axis=2, tiled=True)  143 us
    psum x1, blocking collectives, shards(): window_score = lax.psum(partial_score, ('seq', 'ch'))  76.7 us
    ppermute x12, starting transfers between devices, passed_along(): return lax.ppermute(value, axis, pairs)  39.3 us
    ppermute x12, waiting for transfers between devices, passed_along(): return lax.ppermute(value, axis, pairs)  30.9 us
  transfers between devices with their start and end apart: 31, of which 26 were waited for; matrix products, arithmetic and copies ran while one was open for 3% of the time, Pallas kernels for 0%

commit v1 on v0

v1 whole, which is shorter than its diff:
```python
import functools

import jax
import jax.numpy as jnp
from jax import lax
from jax.experimental import pallas as pl
from jax.experimental.pallas import tpu as pltpu
from jax.sharding import PartitionSpec as P

LAYERS = 5
WIN = 16
STEPS = (1, 4, 8, 16, 32)
MESH = pl.DeviceIdType.MESH
F32 = jnp.float32
BF16 = jnp.bfloat16
HIGH = lax.Precision.HIGHEST
NX, NY, NZ, NS, NC = 4, 4, 8, 32, 8
T = 256
C = 768
CX = 192
CD = 96
NW = 512
NL = 512
KO = 3 * CD
CZ = 24
ROOT = 0.7978845608028654
CUBE = 0.044715


def nt(a, b, **kw):
    return lax.dot_general(a, b, (((1,), (1,)), ((), ())), preferred_element_type=F32, **kw)


def tn(a, b):
    return lax.dot_general(a, b, (((0,), (0,)), ((), ())), preferred_element_type=F32)


def from_low(v, d):
    lane = lax.broadcasted_iota(jnp.int32, v.shape, 1)
    return jnp.where(lane >= d, pltpu.roll(v, d, 1), 0.0)


def from_high(v, d):
    lane = lax.broadcasted_iota(jnp.int32, v.shape, 1)
    return jnp.where(lane < v.shape[1] - d, pltpu.roll(v, v.shape[1] - d, 1), 0.0)


def tower(
    genome, stem, weight, cols_own, start, counts, targets,
    score_out, conv_out, stem_out, head_out,
    gen, gsend, grecv,
    stemw, colw, wst, local_sem, psend, precv,
    letters, act, act2, der, asend, arecv, a2send, a2recv,
    sone, ssone, rsone, stwo, sstwo, rstwo,
    part, bsend, brecv, bcomb, bs, br,
    up, upx, us, ur,
    wg, yrecv, ys, yr, zacc, zsend, zrecv, zs, zr,
    rin, rpart, rys, ryr, rzb, rgb, r_ps, r_pr, r_ys, r_yr, r_zs, r_zr, r_gs, r_gr,
):
    s = lax.axis_index("seq")
    c = lax.axis_index("ch")
    y = s // NZ
    z = s % NZ
    x = c // 2
    q = c % 2
    pc = 2 * x + (1 - q)
    pending = []

    def remote(src, dst, ssem, rsem, seq, ch):
        return pltpu.make_async_remote_copy(
            src_ref=src, dst_ref=dst, send_sem=ssem, recv_sem=rsem,
            device_id=(seq, ch), device_id_type=MESH,
        )

    def go(copy):
        copy.start()
        pending.append(copy)
        return copy

    def x_at(j):
        return 2 * ((x + j) % NX) + q

    def y_at(j):
        return ((y + j) % NY) * NZ + z

    def z_at(j):
        return y * NZ + (z + j) % NZ

    mine = pl.ds(pl.multiple_of(CD * q, CD), CD)
    other = pl.ds(pl.multiple_of(CD * (1 - q), CD), CD)

    local = [
        pltpu.make_async_copy(stem, stemw.at[mine], local_sem.at[0]),
        pltpu.make_async_copy(cols_own, colw.at[mine], local_sem.at[1]),
    ]
    for l in range(LAYERS):
        for k in range(3):
            local.append(
                pltpu.make_async_copy(
                    weight.at[l, k], wst.at[l, k + q * (2 - 2 * k), mine],
                    local_sem.at[2 + 3 * l + k],
                )
            )
    for copy in local:
        copy.start()

    barrier = pltpu.get_barrier_semaphore()

    def greet_seq(j, _):
        pl.semaphore_signal(barrier, inc=1, device_id=((s + j) % NS, c), device_id_type=MESH)
        return 0

    def greet_ch(j, _):
        pl.semaphore_signal(barrier, inc=1, device_id=(s, (c + j) % NC), device_id_type=MESH)
        return 0

    lax.fori_loop(1, NS, greet_seq, 0)
    lax.fori_loop(1, NC, greet_ch, 0)
    pl.semaphore_wait(barrier, NS - 1 + NC - 1)

    def gcopy(j):
        to = (s + j) % NS
        return remote(genome.at[to], gen.at[s], gsend.at[j], grecv.at[j], to, c)

    def gstart(j, _):
        gcopy(j).start()
        return 0

    def gwait(j, _):
        gcopy(j).wait_recv()
        return 0

    def gdone(j, _):
        gcopy(j).wait_send()
        return 0

    lax.fori_loop(1, NS, gstart, 0)
    pstem = go(remote(stem, stemw.at[mine], psend.at[0], precv.at[0], s, pc))
    pw = []
    for l in range(LAYERS):
        pw.append([
            go(remote(
                weight.at[l, k], wst.at[l, k + (1 - q) * (2 - 2 * k), mine],
                psend.at[2 + 3 * l + k], precv.at[2 + 3 * l + k], s, pc,
            ))
            for k in range(3)
        ])
    pcol = go(remote(cols_own, colw.at[mine], psend.at[1], precv.at[1], s, pc))

    gen[s] = genome[s]
    row = lax.broadcasted_iota(jnp.int32, (NL, NL), 0)
    col = lax.broadcasted_iota(jnp.int32, (NL, NL), 1)
    target = 4 * (col % 128) + col // 128
    target = jnp.where(q == 0, target, NL - 1 - target)
    order = (row == target).astype(F32).astype(BF16)
    lax.fori_loop(1, NS, gwait, 0)
    bases = gen[...].reshape(T, 128)
    hot = jnp.concatenate([(bases == n).astype(F32).astype(BF16) for n in range(4)], axis=1)
    letters[...] = nt(hot, order).astype(BF16)

    local[0].wait()
    pstem.wait_recv()
    state = nt(stemw[...], letters[...])

    a2 = []
    for l in range(LAYERS):
        d = STEPS[l]
        sq = state * state
        th = jnp.tanh(ROOT * state * (1.0 + CUBE * sq))
        half = 0.5 * (1.0 + th)
        a = (state * half).astype(BF16)
        act[l, x, 0] = a[:CD]
        act[l, x, 1] = a[CD:]

        def ring(slot, h, j, n):
            return go(remote(
                act.at[l, slot, h], act.at[l, slot, h], asend.at[l, n], arecv.at[l, n], s, x_at(j)
            ))

        f0 = ring(x, 0, 1, 0)
        b1 = ring(x, 1, 3, 1)
        f1 = ring(x, 1, 1, 2)
        b0 = ring(x, 0, 3, 3)
        der[l] = half + (0.5 * ROOT) * state * (1.0 - th * th) * (1.0 + (3 * CUBE) * sq)
        f0.wait_recv()
        fr = ring((x + 3) % NX, 0, 1, 4)
        b1.wait_recv()
        br_ = ring((x + 1) % NX, 1, 3, 5)
        for k in range(3):
            local[2 + 3 * l + k].wait()
            pw[l][k].wait_recv()
        f1.wait_recv()
        b0.wait_recv()
        fr.wait_recv()
        br_.wait_recv()
        a2.append(go(remote(act.at[l], act2.at[l], a2send.at[l], a2recv.at[l], s, pc)))
        p = jnp.dot(
            wst[l].reshape(3 * CX, C), act[l].reshape(C, T), preferred_element_type=F32
        )
        state = (
            state + p[CX:2 * CX] + from_low(p[:CX], d) + from_high(p[2 * CX:], d)
        )

    bins = NS * lax.broadcasted_iota(jnp.int32, (T, NW), 0) + s
    begin = start[...]
    member = ((bins >= begin) & (bins < begin + WIN)).astype(F32)
    pooled = jnp.dot(state, member, precision=HIGH, preferred_element_type=F32) / WIN
    local[1].wait()
    pcol.wait_recv()
    columns = colw[...].astype(F32)
    sone[c] = 0.5 * jnp.sum(pooled * columns, axis=0, keepdims=True)

    def one(j):
        to = (c + j) % NC
        return remote(sone.at[c], sone.at[c], ssone.at[j], rsone.at[j], s, to)

    ones = [go(one(j)) for j in range(1, NC)]

    def reduce_start(r, value):
        rin[r] = value
        return go(remote(rin.at[r, other], rpart.at[r], r_ps.at[r], r_pr.at[r], s, pc))

    def reduce_y(r, first):
        first.wait_recv()
        h = rin[r, mine] + rpart[r]
        for j in range(NY):
            rys[r, j] = h[:, 128 * j:128 * (j + 1)]
        return [
            go(remote(rys.at[r, (y + j) % NY], ryr.at[r, j], r_ys.at[r, j], r_yr.at[r, j], y_at(j), c))
            for j in range(1, NY)
        ]

    def reduce_z(r, copies):
        for copy in copies:
            copy.wait_recv()
        total = rys[r, y] + ryr[r, 1] + ryr[r, 2] + ryr[r, 3]
        rzb[r, z] = total.astype(BF16)
        return [
            go(remote(rzb.at[r, z], rzb.at[r, z], r_zs.at[r, j], r_zr.at[r, j], z_at(j), c))
            for j in range(1, NZ)
        ]

    def reduce_g(r, copies):
        for copy in copies:
            copy.wait_recv()
        total = rzb[r, 0].astype(F32)
        for j in range(1, NZ):
            total = total + rzb[r, j].astype(F32)
        rgb[r, y] = total
        return [
            go(remote(rgb.at[r, y], rgb.at[r, y], r_gs.at[r, j], r_gr.at[r, j], y_at(j), c))
            for j in range(1, NY)
        ]

    def reduce_end(r, copies):
        for copy in copies:
            copy.wait_recv()
        return jnp.concatenate([rgb[r, j] for j in range(NY)], axis=1)

    for copy in ones:
        copy.wait_recv()
    total = sone[0]
    for j in range(1, NC):
        total = total + sone[j]
    stwo[s] = total

    def two(j):
        to = (s + j) % NS
        return remote(stwo.at[s], stwo.at[s], sstwo.at[j], rstwo.at[j], to, c)

    def two_start(j, _):
        two(j).start()
        return 0

    def two_wait(j, _):
        two(j).wait_recv()
        return 0

    def two_done(j, _):
        two(j).wait_send()
        return 0

    lax.fori_loop(1, NS, two_start, 0)
    pool_copy = reduce_start(0, pooled)
    pool_copies = reduce_y(0, pool_copy)
    lax.fori_loop(1, NS, two_wait, 0)
    score = stwo[0]
    for j in range(1, NS):
        score = score + stwo[j]
    score_out[...] = score
    slope = (jnp.exp(score) - targets[...]) / counts[...]
    grad = nt((0.5 / WIN) * slope * columns, member, precision=HIGH)

    waiting_y = None
    waiting_z = []

    def y_stage(item):
        l, copies = item
        for copy in copies:
            copy.wait_recv()
        own = pl.ds(pl.multiple_of(CX * y, CX), CX)
        total = wg[l, own].astype(F32)
        for j in range(1, NY):
            total = total + yrecv[l, j].astype(F32)
        total = total.reshape(NZ, CZ, KO)
        zacc[l] = total
        zsend[l] = total.astype(BF16)
        sends = [
            go(remote(
                zsend.at[l, (z + j) % NZ], zrecv.at[l, j], zs.at[l, j], zr.at[l, j], z_at(j), c
            ))
            for j in range(1, NZ)
        ]
        waiting_z.append((l, sends))

    def z_stage(item):
        l, copies = item
        for copy in copies:
            copy.wait_recv()
        total = zacc[l, z]
        for j in range(1, NZ):
            total = total + zrecv[l, j].astype(F32)
        conv_out[l] = total

    for l in reversed(range(LAYERS)):
        d = STEPS[l]
        u = grad.astype(BF16)
        up[l] = u
        ucopy = go(remote(up.at[l, other], upx.at[l], us.at[l], ur.at[l], s, pc))
        u = u.astype(F32)
        taps = jnp.concatenate(
            [from_high(u, d).astype(BF16), u.astype(BF16), from_low(u, d).astype(BF16)], axis=0
        )
        p = tn(wst[l].reshape(3 * CX, C), taps)
        part[...] = p
        for i in range(NX):
            for h in range(2):
                at = CX * i + CD * h
                bsend[l, i, h] = p[at:at + CD].astype(BF16)

        def shed(src, n, j):
            return go(remote(src, brecv.at[l, n], bs.at[l, n], br.at[l, n], s, x_at(j)))

        far = (x + 2) % NX
        right = (x + 1) % NX
        left = (x + 3) % NX
        f1 = shed(bsend.at[l, far, 1], 0, 1)
        b0 = shed(bsend.at[l, far, 0], 1, 3)
        f0 = shed(bsend.at[l, right, 0], 2, 1)
        b1 = shed(bsend.at[l, left, 1], 3, 3)
        ucopy.wait_recv()
        a2[l].wait_recv()
        v = up[l, mine].astype(F32)
        w = upx[l].astype(F32)
        vh, vl = from_high(v, d).astype(BF16), from_low(v, d).astype(BF16)
        wh, wl = from_high(w, d).astype(BF16), from_low(w, d).astype(BF16)
        first = q == 0
        own_taps = jnp.concatenate(
            [jnp.where(first, vh, vl), v.astype(BF16), jnp.where(first, vl, vh)], axis=0
        )
        far_taps = jnp.concatenate(
            [jnp.where(first, wl, wh), w.astype(BF16), jnp.where(first, wh, wl)], axis=0
        )
        f1.wait_recv()
        b0.wait_recv()
        at = pl.ds(pl.multiple_of(CX * right + CD, CD), CD)
        bcomb[l, 0] = (part[at] + brecv[l, 0].astype(F32)).astype(BF16)
        fc = shed(bcomb.at[l, 0], 4, 1)
        at = pl.ds(pl.multiple_of(CX * left, CD), CD)
        bcomb[l, 1] = (part[at] + brecv[l, 1].astype(F32)).astype(BF16)
        bc = shed(bcomb.at[l, 1], 5, 3)

        g = nt(act[l].reshape(C, T), own_taps) + nt(act2[l].reshape(C, T), far_taps)
        wg[l] = g.astype(BF16)
        ysends = [
            go(remote(
                wg.at[l, pl.ds(pl.multiple_of(CX * ((y + j) % NY), CX), CX)], yrecv.at[l, j],
                ys.at[l, j], yr.at[l, j], y_at(j), c,
            ))
            for j in range(1, NY)
        ]
        if waiting_y is not None:
            y_stage(waiting_y)
        waiting_y = (l, ysends)
        if len(waiting_z) > 1:
            z_stage(waiting_z.pop(0))
        if l == LAYERS - 1:
            pool_copies = reduce_z(0, pool_copies)
        if l == LAYERS - 3:
            pool_copies = reduce_g(0, pool_copies)
        f0.wait_recv()
        b1.wait_recv()
        fc.wait_recv()
        bc.wait_recv()
        own0 = part[pl.ds(pl.multiple_of(CX * x, CD), CD)]
        own1 = part[pl.ds(pl.multiple_of(CX * x + CD, CD), CD)]
        low = own0 + brecv[l, 2].astype(F32) + brecv[l, 5].astype(F32)
        high = own1 + brecv[l, 3].astype(F32) + brecv[l, 4].astype(F32)
        grad = grad + jnp.concatenate([low, high], axis=0) * der[l]

    stem_copy = reduce_start(
        1, jnp.dot(grad.astype(BF16), letters[...], preferred_element_type=F32)
    )
    stem_copies = reduce_y(1, stem_copy)
    y_stage(waiting_y)
    z_stage(waiting_z.pop(0))
    total = reduce_end(0, pool_copies)
    head_out[...] = 0.5 * slope * total
    stem_copies = reduce_z(1, stem_copies)
    while waiting_z:
        z_stage(waiting_z.pop(0))
    stem_copies = reduce_g(1, stem_copies)
    stem_out[...] = reduce_end(1, stem_copies)

    lax.fori_loop(1, NS, gdone, 0)
    lax.fori_loop(1, NS, two_done, 0)
    for copy in pending:
        copy.wait_send()


def shards(
    genome, stem_weight, dilated_filter_weight, head_weight, window_start, window_track, targets
):
    bins = genome.reshape(T // NS, NS, 128).transpose(1, 0, 2)
    columns = jnp.take(head_weight, window_track, axis=1)
    counts = jnp.sum(
        (window_track[:, None] == window_track[None, :]).astype(F32), axis=0, keepdims=True
    )
    dma = pltpu.SemaphoreType.DMA
    V = pltpu.VMEM
    scratch = [
        V((NS, T // NS, 128), jnp.int32), dma((NS,)), dma((NS,)),
        V((CX, NL), BF16), V((CX, NW), BF16), V((LAYERS, 3, CX, C), BF16),
        dma((17,)), dma((17,)), dma((17,)),
        V((T, NL), BF16),
        V((LAYERS, NX, 2, CD, T), BF16), V((LAYERS, NX, 2, CD, T), BF16),
        V((LAYERS, CX, T), F32), dma((LAYERS, 6)), dma((LAYERS, 6)),
        dma((LAYERS,)), dma((LAYERS,)),
        V((NC, 1, NW), F32), dma((NC,)), dma((NC,)),
        V((NS, 1, NW), F32), dma((NS,)), dma((NS,)),
        V((C, T), F32), V((LAYERS, NX, 2, CD, T), BF16), V((LAYERS, 6, CD, T), BF16),
        V((LAYERS, 2, CD, T), BF16), dma((LAYERS, 6)), dma((LAYERS, 6)),
        V((LAYERS, CX, T), BF16), V((LAYERS, CD, T), BF16), dma((LAYERS,)), dma((LAYERS,)),
        V((LAYERS, C, KO), BF16), V((LAYERS, NY, CX, KO), BF16),
        dma((LAYERS, NY)), dma((LAYERS, NY)),
        V((LAYERS, NZ, CZ, KO), F32), V((LAYERS, NZ, CZ, KO), BF16),
        V((LAYERS, NZ, CZ, KO), BF16), dma((LAYERS, NZ)), dma((LAYERS, NZ)),
        V((2, CX, NW), F32), V((2, CD, NW), F32), V((2, NY, CD, 128), F32),
        V((2, NY, CD, 128), F32), V((2, NZ, CD, 128), BF16), V((2, NY, CD, 128), F32),
        dma((2,)), dma((2,)), dma((2, NY)), dma((2, NY)), dma((2, NZ)), dma((2, NZ)),
        dma((2, NY)), dma((2, NY)),
    ]
    vm = pl.BlockSpec(memory_space=pltpu.VMEM)
    hbm = pl.BlockSpec(memory_space=pl.ANY)
    score, conv, stem_grad, terms = pl.pallas_call(
        tower,
        out_shape=(
            jax.ShapeDtypeStruct((1, NW), F32),
            jax.ShapeDtypeStruct((LAYERS, CZ, KO), F32),
            jax.ShapeDtypeStruct((CD, NL), F32),
            jax.ShapeDtypeStruct((CD, NW), F32),
        ),
        in_specs=[vm, hbm, hbm, hbm, vm, vm, vm],
        out_specs=(vm, vm, vm, vm),
        scratch_shapes=scratch,
        compiler_params=pltpu.CompilerParams(
            collective_id=0, has_side_effects=True, vmem_limit_bytes=60 * 1024 * 1024
        ),
    )(
        bins, stem_weight, dilated_filter_weight, columns,
        window_start.reshape(1, NW), counts, targets.reshape(1, NW),
    )
    conv_grad = conv.reshape(LAYERS, CZ, 3, CD).transpose(0, 2, 3, 1)
    head_grad = jnp.zeros(head_weight.shape, F32).at[:, window_track].add(terms)
    return (score.reshape(NW), conv_grad, stem_grad, head_grad)


def solution(mesh):
    return jax.shard_map(
        shards,
        mesh=mesh,
        in_specs=(
            P("seq", None),
            P("ch", None),
            P(None, None, "ch", None),
            P("ch", None),
            P(),
            P(),
            P(),
        ),
        out_specs=(P(), P(None, None, "ch", "seq"), P("ch", None), P("ch", None)),
        check_vma=False,
    )
```

time: 822 us -> 159 us (0.19)
  waiting for transfers between devices: 594 us -> 0 us
  Pallas kernels: 0 us -> 140 us
  blocking collectives: 76.7 us -> 0 us
  starting transfers between devices: 60.7 us -> 0 us
  matrix products: 32.7 us -> 0 us
  local copies, waits for them, and re-layouts: 26.2 us -> 11.4 us
  between operations: 15.4 us -> 0.71 us
    unnamed x12 -> x0, waiting for transfers between devices: 247 us -> none
    reduce_scatter x5 -> x0, waiting for transfers between devices: 165 us -> none  [shards(): through = lax.psum_scatter(spread, 'ch', scatter_dimension=1, tiled=True)]
    all_gather x5 -> x0, waiting for transfers between devices: 143 us -> none  [shards(): collected_taps = lax.all_gather(resident_taps, 'ch', axis=2, tiled=True)]
    pallas_call x0 -> x1, Pallas kernels: none -> 140 us  [shards(): pl.pallas_call(tower, out_shape=(jax.ShapeDtypeStruct((1, NW), F32), jax....]
    psum x1 -> x0, blocking collectives: 76.7 us -> none  [shards(): window_score = lax.psum(partial_score, ('seq', 'ch'))]
    ppermute x20 -> x0, starting transfers between devices: 60.3 us -> none  [the longest x12 39.3 us: passed_along(): return lax.ppermute(value, axis, pairs)]
    ppermute x20 -> x0, waiting for transfers between devices: 40.2 us -> none  [the longest x12 30.9 us: passed_along(): return lax.ppermute(value, axis, pairs)]
    dot_general x19 -> x0, matrix products: 32.7 us -> none  [the longest x5 11.1 us: shards(): jnp.einsum('nezp,efz->nfp', collected_taps, dilated_filter_weight[current...]
  transfers between devices with their start and end apart: 31 -> 0, of which waited for: 26 -> 0; matrix products, arithmetic and copies ran while one was open for 3% -> 0% of each run, Pallas kernels for 0% -> 0%
where the time goes in v1:
time: 159 us
  Pallas kernels  140 us (88%)
  local copies, waits for them, and re-layouts  11.4 us (7%)
  other arithmetic  6.43 us (4%)
    pallas_call x1, Pallas kernels, shards(): pl.pallas_call(tower, out_shape=(jax.ShapeDtypeStruct((1, NW), F32), jax....  140 us
    unnamed x9, local copies, waits for them, and re-layouts  6.15 us

profile of v1, /device:TPU:1, one launch (start us, length us, event | category | flops | bytes accessed | tf_op | source)
XLA Modules:
  0.0 158.9 jit_solution(4827247075086826530)
XLA Ops:
  0.6 0.7 compare_and_fusion
  1.3 0.7 compare_select_fusion
  2.0 1.5 convert_reduce_fusion
  3.5 1.6 %copy.29 = s32[8,32,128]{2,0,1:T(8,128)} copy(s32[8,32,128]{2,1,0:T(8,128)} %bitcast.15) | data formatting | bytes 262144 | tf_op jit(solution)/shard_map/reshape | solution.py:424
  5.2 2.0 %copy.23 = bf16[96,5313]{0,1:T(8,128)(2,1)S(1)} copy(bf16[96,5313]{1,0:T(8,128)(2,1)} %param.10) | data formatting | bytes 2040192 | tf_op args[3]
  7.2 1.3 gather_fusion
  8.5 0.1 copy.24
  8.7 0.7 select_bitcast_fusion.cols_own
  9.3 140.4 %shard_map.102 = (f32[1,512]{1,0:T(1,128)}, f32[5,24,288]{2,1,0:T(8,128)}, f32[96,512]{1,0:T(8,128)}, f32[96,512]{1,0:T(8,128)}) custom-call(s32[32,8,128]{2,1,0:T(8,128)} %bitcast.13, bf16[96,512]{1,0:T(8,128)(2,1)} %stem.1, bf16[5,3,96,768]{3,2,1,0:T(8,128)(2,1)} %weight.1, bf16[96,512]{1,0:T(8,128)(2,1)} %select_bitcast_fusion.cols_own, ...), custom_call_target="tpu_custom_call" | custom-call | tf_op jit(solution)/shard_map/pallas_call | solution.py:455
  149.7 1.1 reshape.34
  150.8 0.7 copy.26
  151.5 1.0 copy.25
  152.6 2.9 %scatter_custom_fusion = f32[96,5313]{0,1:T(8,128)S(1)} fusion(s32[512]{0:T(512)S(1)} %compare_select_fusion, f32[512,96]{1,0:T(8,128)S(1)} %copy.25, f32[]{:T(128)} %constant.20.clone.1), kind=kCustom, calls=%fused_computation.2 | custom fusion | flops 49152 | bytes 2040196 | tf_op jit(solution)/shard_map/scatter-add | solution.py:474
  155.5 0.0 copy-start.1
  155.5 0.0 copy-start
  155.5 2.2 %copy.27 = f32[96,5313]{1,0:T(8,128)} copy(f32[96,5313]{0,1:T(8,128)S(1)} %scatter_custom_fusion) | data formatting | bytes 4080384
  157.7 0.0 copy-done.1
  157.7 0.6 copy.32
  158.2 0.0 copy-done
  158.3 0.7 copy.33
  (1 shorter events, 0.0 us)
Async XLA Ops:
  155.5 2.2 %copy-start.1 = (f32[1,512]{1,0:T(1,128)S(1)}, f32[1,512]{1,0:T(1,128)}, u32[]{:S(2)}) copy-start(f32[1,512]{1,0:T(1,128)} %get-tuple-element.8) | copy-start | bytes 6148
  155.5 2.8 %copy-start = (f32[96,512]{1,0:T(8,128)S(1)}, f32[96,512]{1,0:T(8,128)}, u32[]{:S(2)}) copy-start(f32[96,512]{1,0:T(8,128)} %get-tuple-element.30) | copy-start | bytes 589828

commit v2 on v1

--- a/solution.py
+++ b/solution.py
@@ -23,6 +23,10 @@
 NL = 512
 KO = 3 * CD
 CZ = 24
+TRACKS = 5313
+CHUNK = 512
+WHOLE = TRACKS // CHUNK
+REST = TRACKS - WHOLE * CHUNK
 ROOT = 0.7978845608028654
 CUBE = 0.044715
 
@@ -46,16 +50,16 @@
 
 
 def tower(
-    genome, stem, weight, cols_own, start, counts, targets,
+    genome, stem, weight, head, start, track, targets,
     score_out, conv_out, stem_out, head_out,
-    gen, gsend, grecv,
+    gbuf, gen, gsend, grecv, headw,
     stemw, colw, wst, local_sem, psend, precv,
     letters, act, act2, der, asend, arecv, a2send, a2recv,
     sone, ssone, rsone, stwo, sstwo, rstwo,
     part, bsend, brecv, bcomb, bs, br,
     up, upx, us, ur,
     wg, yrecv, ys, yr, zacc, zsend, zrecv, zs, zr,
-    rin, rpart, rys, ryr, rzb, rgb, r_ps, r_pr, r_ys, r_yr, r_zs, r_zr, r_gs, r_gr,
+    rys, ryr, rzb, rgb, r_ys, r_yr, r_zs, r_zr, r_gs, r_gr, thirds,
 ):
     s = lax.axis_index("seq")
     c = lax.axis_index("ch")
@@ -66,6 +70,13 @@
     pc = 2 * x + (1 - q)
     pending = []
 
+    def one_hot(base, width):
+        ids = lax.broadcasted_iota(jnp.int32, (width, NW), 0) + base
+        return (ids == track[...]).astype(F32).astype(BF16)
+
+    def chunk(i):
+        return pl.ds(pl.multiple_of(i * CHUNK, CHUNK), CHUNK)
+
     def remote(src, dst, ssem, rsem, seq, ch):
         return pltpu.make_async_remote_copy(
             src_ref=src, dst_ref=dst, send_sem=ssem, recv_sem=rsem,
@@ -77,6 +88,10 @@
         pending.append(copy)
         return copy
 
+    def lead(copy):
+        pending[:] = [p for p in pending if p is not copy]
+        copy.wait_send()
+
     def x_at(j):
         return 2 * ((x + j) % NX) + q
 
@@ -91,7 +106,7 @@
 
     local = [
         pltpu.make_async_copy(stem, stemw.at[mine], local_sem.at[0]),
-        pltpu.make_async_copy(cols_own, colw.at[mine], local_sem.at[1]),
+        pltpu.make_async_copy(head, headw, local_sem.at[1]),
     ]
     for l in range(LAYERS):
         for k in range(3):
@@ -116,11 +131,15 @@
 
     lax.fori_loop(1, NS, greet_seq, 0)
     lax.fori_loop(1, NC, greet_ch, 0)
-    pl.semaphore_wait(barrier, NS - 1 + NC - 1)
+    for j in range(1, NY):
+        pl.semaphore_signal(barrier, inc=1, device_id=(y_at(j), pc), device_id_type=MESH)
+    for r in range(NS):
+        gbuf[r] = genome[pl.ds(r, T // NS, stride=NS), :]
+    pl.semaphore_wait(barrier, NS - 1 + NC - 1 + NY - 1)
 
     def gcopy(j):
         to = (s + j) % NS
-        return remote(genome.at[to], gen.at[s], gsend.at[j], grecv.at[j], to, c)
+        return remote(gbuf.at[to], gen.at[s], gsend.at[j], grecv.at[j], to, c)
 
     def gstart(j, _):
         gcopy(j).start()
@@ -145,9 +164,24 @@
             ))
             for k in range(3)
         ])
-    pcol = go(remote(cols_own, colw.at[mine], psend.at[1], precv.at[1], s, pc))
-
-    gen[s] = genome[s]
+
+    gen[s] = gbuf[s]
+    local[1].wait()
+
+    def pick(i, total):
+        return total + jnp.dot(
+            headw[:, chunk(i)], one_hot(i * CHUNK, CHUNK), preferred_element_type=F32
+        )
+
+    picked = lax.fori_loop(0, WHOLE, pick, jnp.zeros((CD, NW), F32))
+    picked = picked + jnp.dot(
+        headw[:, WHOLE * CHUNK:], one_hot(WHOLE * CHUNK, REST), preferred_element_type=F32
+    )
+    colw[mine] = picked.astype(BF16)
+    pcol = go(remote(colw.at[mine], colw.at[mine], psend.at[1], precv.at[1], s, pc))
+    tracks = jnp.broadcast_to(track[...].astype(F32), (8, NW))
+    across = jnp.transpose(tracks)[:, :1]
+    counts = jnp.sum((across == tracks[:1]).astype(F32), axis=0, keepdims=True)
     row = lax.broadcasted_iota(jnp.int32, (NL, NL), 0)
     col = lax.broadcasted_iota(jnp.int32, (NL, NL), 1)
     target = 4 * (col % 128) + col // 128
@@ -162,7 +196,9 @@
     pstem.wait_recv()
     state = nt(stemw[...], letters[...])
 
-    a2 = []
+    def share(l):
+        return go(remote(act.at[l], act2.at[l], a2send.at[l], a2recv.at[l], s, pc))
+
     for l in range(LAYERS):
         d = STEPS[l]
         sq = state * state
@@ -179,9 +215,11 @@
 
         f0 = ring(x, 0, 1, 0)
         b1 = ring(x, 1, 3, 1)
+        der[l] = half + (0.5 * ROOT) * state * (1.0 - th * th) * (1.0 + (3 * CUBE) * sq)
+        lead(f0)
         f1 = ring(x, 1, 1, 2)
+        lead(b1)
         b0 = ring(x, 0, 3, 3)
-        der[l] = half + (0.5 * ROOT) * state * (1.0 - th * th) * (1.0 + (3 * CUBE) * sq)
         f0.wait_recv()
         fr = ring((x + 3) % NX, 0, 1, 4)
         b1.wait_recv()
@@ -193,7 +231,6 @@
         b0.wait_recv()
         fr.wait_recv()
         br_.wait_recv()
-        a2.append(go(remote(act.at[l], act2.at[l], a2send.at[l], a2recv.at[l], s, pc)))
         p = jnp.dot(
             wst[l].reshape(3 * CX, C), act[l].reshape(C, T), preferred_element_type=F32
         )
@@ -205,7 +242,6 @@
     begin = start[...]
     member = ((bins >= begin) & (bins < begin + WIN)).astype(F32)
     pooled = jnp.dot(state, member, precision=HIGH, preferred_element_type=F32) / WIN
-    local[1].wait()
     pcol.wait_recv()
     columns = colw[...].astype(F32)
     sone[c] = 0.5 * jnp.sum(pooled * columns, axis=0, keepdims=True)
@@ -216,24 +252,24 @@
 
     ones = [go(one(j)) for j in range(1, NC)]
 
-    def reduce_start(r, value):
-        rin[r] = value
-        return go(remote(rin.at[r, other], rpart.at[r], r_ps.at[r], r_pr.at[r], s, pc))
-
-    def reduce_y(r, first):
-        first.wait_recv()
-        h = rin[r, mine] + rpart[r]
-        for j in range(NY):
-            rys[r, j] = h[:, 128 * j:128 * (j + 1)]
+    def reduce_y(r, value):
+        for i in range(2):
+            for j in range(NY):
+                rys[r, i, j] = value[CD * i:CD * (i + 1), 128 * j:128 * (j + 1)].astype(BF16)
         return [
-            go(remote(rys.at[r, (y + j) % NY], ryr.at[r, j], r_ys.at[r, j], r_yr.at[r, j], y_at(j), c))
-            for j in range(1, NY)
+            go(remote(
+                rys.at[r, (q + i) % 2, (y + j) % NY], ryr.at[r, NY * i + j],
+                r_ys.at[r, NY * i + j], r_yr.at[r, NY * i + j], y_at(j), 2 * x + (q + i) % 2,
+            ))
+            for j in range(NY) for i in range(2) if i + j > 0
         ]
 
     def reduce_z(r, copies):
         for copy in copies:
             copy.wait_recv()
-        total = rys[r, y] + ryr[r, 1] + ryr[r, 2] + ryr[r, 3]
+        total = rys[r, q, y].astype(F32)
+        for i in range(1, 2 * NY):
+            total = total + ryr[r, i].astype(F32)
         rzb[r, z] = total.astype(BF16)
         return [
             go(remote(rzb.at[r, z], rzb.at[r, z], r_zs.at[r, j], r_zr.at[r, j], z_at(j), c))
@@ -281,14 +317,14 @@
         return 0
 
     lax.fori_loop(1, NS, two_start, 0)
-    pool_copy = reduce_start(0, pooled)
-    pool_copies = reduce_y(0, pool_copy)
+    pool_copies = reduce_y(0, pooled)
+    a2 = {4: share(4), 3: share(3)}
     lax.fori_loop(1, NS, two_wait, 0)
     score = stwo[0]
     for j in range(1, NS):
         score = score + stwo[j]
     score_out[...] = score
-    slope = (jnp.exp(score) - targets[...]) / counts[...]
+    slope = (jnp.exp(score) - targets[...]) / counts
     grad = nt((0.5 / WIN) * slope * columns, member, precision=HIGH)
 
     waiting_y = None
@@ -320,7 +356,18 @@
         total = zacc[l, z]
         for j in range(1, NZ):
             total = total + zrecv[l, j].astype(F32)
-        conv_out[l] = total
+        conv_out[l] = jnp.transpose(total).reshape(3, CD, CZ)
+
+    def place(first, last):
+        def body(i, _):
+            head_out[:, chunk(i)] = spread_out(one_hot(i * CHUNK, CHUNK))
+            return 0
+
+        lax.fori_loop(first, last, body, 0)
+
+    def spread_out(hot):
+        out = nt(thirds[...], hot)
+        return out[:CD] + out[CD:2 * CD] + out[2 * CD:]
 
     for l in reversed(range(LAYERS)):
         d = STEPS[l]
@@ -346,21 +393,34 @@
         left = (x + 3) % NX
         f1 = shed(bsend.at[l, far, 1], 0, 1)
         b0 = shed(bsend.at[l, far, 0], 1, 3)
+        if l >= 2:
+            a2[l - 2] = share(l - 2)
+        first = q == 0
+        v = up[l, mine].astype(F32)
+        vh, vl = from_high(v, d).astype(BF16), from_low(v, d).astype(BF16)
+        own_taps = jnp.concatenate(
+            [jnp.where(first, vh, vl), v.astype(BF16), jnp.where(first, vl, vh)], axis=0
+        )
+        g = nt(act[l].reshape(C, T), own_taps)
+        lead(f1)
         f0 = shed(bsend.at[l, right, 0], 2, 1)
+        lead(b0)
         b1 = shed(bsend.at[l, left, 1], 3, 3)
         ucopy.wait_recv()
         a2[l].wait_recv()
-        v = up[l, mine].astype(F32)
         w = upx[l].astype(F32)
-        vh, vl = from_high(v, d).astype(BF16), from_low(v, d).astype(BF16)
         wh, wl = from_high(w, d).astype(BF16), from_low(w, d).astype(BF16)
-        first = q == 0
-        own_taps = jnp.concatenate(
-            [jnp.where(first, vh, vl), v.astype(BF16), jnp.where(first, vl, vh)], axis=0
-        )
         far_taps = jnp.concatenate(
             [jnp.where(first, wl, wh), w.astype(BF16), jnp.where(first, wh, wl)], axis=0
         )
+        wg[l] = (g + nt(act2[l].reshape(C, T), far_taps)).astype(BF16)
+        ysends = [
+            go(remote(
+                wg.at[l, pl.ds(pl.multiple_of(CX * ((y + j) % NY), CX), CX)], yrecv.at[l, j],
+                ys.at[l, j], yr.at[l, j], y_at(j), c,
+            ))
+            for j in range(1, NY)
+        ]
         f1.wait_recv()
         b0.wait_recv()
         at = pl.ds(pl.multiple_of(CX * right + CD, CD), CD)
@@ -369,16 +429,6 @@
         at = pl.ds(pl.multiple_of(CX * left, CD), CD)
         bcomb[l, 1] = (part[at] + brecv[l, 1].astype(F32)).astype(BF16)
         bc = shed(bcomb.at[l, 1], 5, 3)
-
-        g = nt(act[l].reshape(C, T), own_taps) + nt(act2[l].reshape(C, T), far_taps)
-        wg[l] = g.astype(BF16)
-        ysends = [
-            go(remote(
-                wg.at[l, pl.ds(pl.multiple_of(CX * ((y + j) % NY), CX), CX)], yrecv.at[l, j],
-                ys.at[l, j], yr.at[l, j], y_at(j), c,
-            ))
-            for j in range(1, NY)
-        ]
         if waiting_y is not None:
             y_stage(waiting_y)
         waiting_y = (l, ysends)
@@ -386,8 +436,18 @@
             z_stage(waiting_z.pop(0))
         if l == LAYERS - 1:
             pool_copies = reduce_z(0, pool_copies)
+        if l == LAYERS - 2:
+            pool_copies = reduce_g(0, pool_copies)
         if l == LAYERS - 3:
-            pool_copies = reduce_g(0, pool_copies)
+            terms = 0.5 * slope * reduce_end(0, pool_copies)
+            for i in range(3):
+                piece = terms.astype(BF16)
+                thirds[CD * i:CD * (i + 1)] = piece
+                terms = terms - piece.astype(F32)
+            place(0, WHOLE // 2)
+        if l == LAYERS - 4:
+            place(WHOLE // 2, WHOLE)
+            head_out[:, WHOLE * CHUNK:] = spread_out(one_hot(WHOLE * CHUNK, REST))
         f0.wait_recv()
         b1.wait_recv()
         fc.wait_recv()
@@ -398,14 +458,11 @@
         high = own1 + brecv[l, 3].astype(F32) + brecv[l, 4].astype(F32)
         grad = grad + jnp.concatenate([low, high], axis=0) * der[l]
 
-    stem_copy = reduce_start(
+    stem_copies = reduce_y(
         1, jnp.dot(grad.astype(BF16), letters[...], preferred_element_type=F32)
     )
-    stem_copies = reduce_y(1, stem_copy)
     y_stage(waiting_y)
     z_stage(waiting_z.pop(0))
-    total = reduce_end(0, pool_copies)
-    head_out[...] = 0.5 * slope * total
     stem_copies = reduce_z(1, stem_copies)
     while waiting_z:
         z_stage(waiting_z.pop(0))
@@ -421,15 +478,11 @@
 def shards(
     genome, stem_weight, dilated_filter_weight, head_weight, window_start, window_track, targets
 ):
-    bins = genome.reshape(T // NS, NS, 128).transpose(1, 0, 2)
-    columns = jnp.take(head_weight, window_track, axis=1)
-    counts = jnp.sum(
-        (window_track[:, None] == window_track[None, :]).astype(F32), axis=0, keepdims=True
-    )
     dma = pltpu.SemaphoreType.DMA
     V = pltpu.VMEM
     scratch = [
-        V((NS, T // NS, 128), jnp.int32), dma((NS,)), dma((NS,)),
+        V((NS, T // NS, 128), jnp.int32), V((NS, T // NS, 128), jnp.int32), dma((NS,)), dma((NS,)),
+        V((CD, TRACKS), BF16),
         V((CX, NL), BF16), V((CX, NW), BF16), V((LAYERS, 3, CX, C), BF16),
         dma((17,)), dma((17,)), dma((17,)),
         V((T, NL), BF16),
@@ -445,20 +498,20 @@
         dma((LAYERS, NY)), dma((LAYERS, NY)),
         V((LAYERS, NZ, CZ, KO), F32), V((LAYERS, NZ, CZ, KO), BF16),
         V((LAYERS, NZ, CZ, KO), BF16), dma((LAYERS, NZ)), dma((LAYERS, NZ)),
-        V((2, CX, NW), F32), V((2, CD, NW), F32), V((2, NY, CD, 128), F32),
-        V((2, NY, CD, 128), F32), V((2, NZ, CD, 128), BF16), V((2, NY, CD, 128), F32),
-        dma((2,)), dma((2,)), dma((2, NY)), dma((2, NY)), dma((2, NZ)), dma((2, NZ)),
-        dma((2, NY)), dma((2, NY)),
+        V((2, 2, NY, CD, 128), BF16), V((2, 2 * NY, CD, 128), BF16),
+        V((2, NZ, CD, 128), BF16), V((2, NY, CD, 128), F32),
+        dma((2, 2 * NY)), dma((2, 2 * NY)), dma((2, NZ)), dma((2, NZ)),
+        dma((2, NY)), dma((2, NY)), V((KO, NW), BF16),
     ]
     vm = pl.BlockSpec(memory_space=pltpu.VMEM)
     hbm = pl.BlockSpec(memory_space=pl.ANY)
-    score, conv, stem_grad, terms = pl.pallas_call(
+    score, conv_grad, stem_grad, head_grad = pl.pallas_call(
         tower,
         out_shape=(
             jax.ShapeDtypeStruct((1, NW), F32),
-            jax.ShapeDtypeStruct((LAYERS, CZ, KO), F32),
+            jax.ShapeDtypeStruct((LAYERS, 3, CD, CZ), F32),
             jax.ShapeDtypeStruct((CD, NL), F32),
-            jax.ShapeDtypeStruct((CD, NW), F32),
+            jax.ShapeDtypeStruct((CD, TRACKS), F32),
         ),
         in_specs=[vm, hbm, hbm, hbm, vm, vm, vm],
         out_specs=(vm, vm, vm, vm),
@@ -467,11 +520,9 @@
             collective_id=0, has_side_effects=True, vmem_limit_bytes=60 * 1024 * 1024
         ),
     )(
-        bins, stem_weight, dilated_filter_weight, columns,
-        window_start.reshape(1, NW), counts, targets.reshape(1, NW),
+        genome, stem_weight, dilated_filter_weight, head_weight,
+        window_start.reshape(1, NW), window_track.reshape(1, NW), targets.reshape(1, NW),
     )
-    conv_grad = conv.reshape(LAYERS, CZ, 3, CD).transpose(0, 2, 3, 1)
-    head_grad = jnp.zeros(head_weight.shape, F32).at[:, window_track].add(terms)
     return (score.reshape(NW), conv_grad, stem_grad, head_grad)
 
 

time: 159 us -> 146 us (0.918)
  other arithmetic: 6.43 us -> 0 us
  Pallas kernels: 140 us -> 136 us
  local copies, waits for them, and re-layouts: 11.4 us -> 7.91 us
    pallas_call x1, Pallas kernels: 140 us -> 136 us  [shards(): pl.pallas_call(tower, out_shape=(jax.ShapeDtypeStruct((1, NW), F32), jax....]
    scatter-add x1 -> x0, other arithmetic: 2.88 us -> none  [shards(): head_grad = jnp.zeros(head_weight.shape, F32).at[:, window_track].add(terms)]
    reshape x2 -> x0, local copies, waits for them, and re-layouts: 2.72 us -> none  [the longest x1 1.64 us: shards(): bins = genome.reshape(T // NS, NS, 128).transpose(1, 0, 2)]
    unnamed x9 -> x4, local copies, waits for them, and re-layouts: 6.15 us -> 7.91 us
where the time goes in v2:
time: 146 us; the launch traced here: 145 us
  Pallas kernels  136 us (93%)
  local copies, waits for them, and re-layouts  7.91 us (5%)
    pallas_call x1, Pallas kernels, shards(): pl.pallas_call(tower, out_shape=(jax.ShapeDtypeStruct((1, NW), F32), jax....  136 us
    unnamed x4, local copies, waits for them, and re-layouts  7.91 us

profile of v2, /device:TPU:1, one launch (start us, length us, event | category | flops | bytes accessed | tf_op | source)
XLA Modules:
  0.0 144.9 jit_solution(1097647836690418371)
XLA Ops:
  0.6 136.4 %shard_map.102 = (f32[1,512]{1,0:T(1,128)}, f32[5,3,96,24]{3,2,1,0:T(8,128)}, f32[96,512]{1,0:T(8,128)}, f32[96,5313]{1,0:T(8,128)}) custom-call(s32[256,128]{1,0:T(8,128)} %genome.1, bf16[96,512]{1,0:T(8,128)(2,1)} %stem.1, bf16[5,3,96,768]{3,2,1,0:T(8,128)(2,1)} %weight.1, bf16[96,5313]{1,0:T(8,128)(2,1)} %head.1, s32[1,512]{1,0:T(1,128)} %bitcast.4, ...), custom_call_target="tpu_custom_call" | custom-call | tf_op jit(solution)/shard_map/pallas_call | solution.py:508
  137.0 2.0 %copy.11 = f32[5,3,96,24]{2,3,1,0:T(8,128)} copy(f32[5,3,96,24]{3,2,1,0:T(8,128)} %get-tuple-element.13) | data formatting | bytes 276480
  139.1 1.2 copy.15
  140.3 1.6 %copy.16 = f32[96,512]{1,0:T(8,128)} copy(f32[96,512]{1,0:T(8,128)} %get-tuple-element.22) | data formatting | bytes 393216
  141.9 3.0 %copy.17 = f32[96,5313]{1,0:T(8,128)} copy(f32[96,5313]{1,0:T(8,128)} %get-tuple-element.23) | data formatting | bytes 4080384

commit v3 on v2

--- a/solution.py
+++ b/solution.py
@@ -356,7 +356,8 @@
         total = zacc[l, z]
         for j in range(1, NZ):
             total = total + zrecv[l, j].astype(F32)
-        conv_out[l] = jnp.transpose(total).reshape(3, CD, CZ)
+        for k in range(3):
+            conv_out[l, k] = total[:, CD * k:CD * (k + 1)]
 
     def place(first, last):
         def body(i, _):
@@ -475,6 +476,23 @@
         copy.wait_send()
 
 
+def deliver(score, conv, stem, head, score_to, conv_to, stem_to, head_to, sem):
+    copies = [
+        pltpu.make_async_copy(
+            head.at[pl.ds(24 * i, 24)], head_to.at[pl.ds(24 * i, 24)], sem.at[2 + LAYERS + i]
+        )
+        for i in range(4)
+    ]
+    for l in range(LAYERS):
+        copies.append(pltpu.make_async_copy(conv.at[l], conv_to.at[l], sem.at[2 + l]))
+    copies.append(pltpu.make_async_copy(stem, stem_to, sem.at[0]))
+    copies.append(pltpu.make_async_copy(score, score_to, sem.at[1]))
+    for copy in copies:
+        copy.start()
+    for copy in copies:
+        copy.wait()
+
+
 def shards(
     genome, stem_weight, dilated_filter_weight, head_weight, window_start, window_track, targets
 ):
@@ -508,10 +526,7 @@
     score, conv_grad, stem_grad, head_grad = pl.pallas_call(
         tower,
         out_shape=(
-            jax.ShapeDtypeStruct((1, NW), F32),
-            jax.ShapeDtypeStruct((LAYERS, 3, CD, CZ), F32),
-            jax.ShapeDtypeStruct((CD, NL), F32),
-            jax.ShapeDtypeStruct((CD, TRACKS), F32),
+            V((1, NW), F32), V((LAYERS, 3, CZ, CD), F32), V((CD, NL), F32), V((CD, TRACKS), F32),
         ),
         in_specs=[vm, hbm, hbm, hbm, vm, vm, vm],
         out_specs=(vm, vm, vm, vm),
@@ -523,7 +538,15 @@
         genome, stem_weight, dilated_filter_weight, head_weight,
         window_start.reshape(1, NW), window_track.reshape(1, NW), targets.reshape(1, NW),
     )
-    return (score.reshape(NW), conv_grad, stem_grad, head_grad)
+    results = (score, conv_grad, stem_grad, head_grad)
+    score, conv_grad, stem_grad, head_grad = pl.pallas_call(
+        deliver,
+        out_shape=tuple(jax.ShapeDtypeStruct(r.shape, F32) for r in results),
+        in_specs=[vm] * 4,
+        out_specs=(hbm,) * 4,
+        scratch_shapes=[dma((2 + LAYERS + 4,))],
+    )(*[pltpu.with_memory_space_constraint(r, pltpu.VMEM) for r in results])
+    return (score.reshape(NW), conv_grad.transpose(0, 1, 3, 2), stem_grad, head_grad)
 
 
 def solution(mesh):

time: 146 us -> 138 us (0.945)
  local copies, waits for them, and re-layouts: 7.91 us -> 0 us
    unnamed x4 -> x0, local copies, waits for them, and re-layouts: 7.91 us -> none
    pallas_call x1 -> x2, Pallas kernels: 136 us -> 136 us  [the longest x1 135 us: shards(): pl.pallas_call(tower, out_shape=(V((1, NW), F32), V((LAYERS, 3, CZ, CD),...]
where the time goes in v3:
time: 138 us; the launch traced here: 137 us
  Pallas kernels  136 us (99%)
    pallas_call x1, Pallas kernels, shards(): pl.pallas_call(tower, out_shape=(V((1, NW), F32), V((LAYERS, 3, CZ, CD),...  135 us

profile of v3, /device:TPU:1, one launch (start us, length us, event | category | flops | bytes accessed | tf_op | source)
XLA Modules:
  0.0 137.1 jit_solution(12214009730224133618)
XLA Ops:
  0.6 134.7 %shard_map.102 = (f32[1,512]{1,0:T(1,128)S(1)}, f32[5,3,24,96]{3,2,1,0:T(8,128)S(1)}, f32[96,512]{1,0:T(8,128)S(1)}, f32[96,5313]{1,0:T(8,128)S(1)}) custom-call(s32[256,128]{1,0:T(8,128)} %genome.1, bf16[96,512]{1,0:T(8,128)(2,1)} %stem.1, bf16[5,3,96,768]{3,2,1,0:T(8,128)(2,1)} %weight.1, bf16[96,5313]{1,0:T(8,128)(2,1)} %head.1, s32[1,512]{1,0:T(1,128)} %bitcast.5, ...), custom_call_target="tpu_custom_call" | custom-call | tf_op jit(solution)/shard_map/pallas_call | solution.py:526
  135.4 1.5 %shard_map.103 = (f32[1,512]{1,0:T(1,128)}, f32[5,3,24,96]{3,2,1,0:T(8,128)}, f32[96,512]{1,0:T(8,128)}, f32[96,5313]{1,0:T(8,128)}) custom-call(f32[1,512]{1,0:T(1,128)S(1)} %get-tuple-element.12.score, f32[5,3,24,96]{3,2,1,0:T(8,128)S(1)} %get-tuple-element.13.conv, f32[96,512]{1,0:T(8,128)S(1)} %get-tuple-element.14.stem, ...), custom_call_target="tpu_custom_call" | custom-call | tf_op jit(solution)/shard_map/pallas_call | solution.py:542

commit v4 on v3

--- a/solution.py
+++ b/solution.py
@@ -51,7 +51,8 @@
 
 def tower(
     genome, stem, weight, head, start, track, targets,
-    score_out, conv_out, stem_out, head_out,
+    score_to, conv_to, stem_to, head_to,
+    score_out, conv_out, stem_out, head_out, out_sem,
     gbuf, gen, gsend, grecv, headw,
     stemw, colw, wst, local_sem, psend, precv,
     letters, act, act2, der, asend, arecv, a2send, a2recv,
@@ -69,6 +70,12 @@
     q = c % 2
     pc = 2 * x + (1 - q)
     pending = []
+    leaving = []
+
+    def leave(src, dst, n):
+        copy = pltpu.make_async_copy(src, dst, out_sem.at[n])
+        copy.start()
+        leaving.append(copy)
 
     def one_hot(base, width):
         ids = lax.broadcasted_iota(jnp.int32, (width, NW), 0) + base
@@ -324,6 +331,7 @@
     for j in range(1, NS):
         score = score + stwo[j]
     score_out[...] = score
+    leave(score_out, score_to, LAYERS)
     slope = (jnp.exp(score) - targets[...]) / counts
     grad = nt((0.5 / WIN) * slope * columns, member, precision=HIGH)
 
@@ -358,6 +366,7 @@
             total = total + zrecv[l, j].astype(F32)
         for k in range(3):
             conv_out[l, k] = total[:, CD * k:CD * (k + 1)]
+        leave(conv_out.at[l], conv_to.at[l], l)
 
     def place(first, last):
         def body(i, _):
@@ -449,6 +458,7 @@
         if l == LAYERS - 4:
             place(WHOLE // 2, WHOLE)
             head_out[:, WHOLE * CHUNK:] = spread_out(one_hot(WHOLE * CHUNK, REST))
+            leave(head_out, head_to, LAYERS + 1)
         f0.wait_recv()
         b1.wait_recv()
         fc.wait_recv()
@@ -469,11 +479,14 @@
         z_stage(waiting_z.pop(0))
     stem_copies = reduce_g(1, stem_copies)
     stem_out[...] = reduce_end(1, stem_copies)
+    leave(stem_out, stem_to, LAYERS + 2)
 
     lax.fori_loop(1, NS, gdone, 0)
     lax.fori_loop(1, NS, two_done, 0)
     for copy in pending:
         copy.wait_send()
+    for copy in leaving:
+        copy.wait()
 
 
 def deliver(score, conv, stem, head, score_to, conv_to, stem_to, head_to, sem):
@@ -498,7 +511,11 @@
 ):
     dma = pltpu.SemaphoreType.DMA
     V = pltpu.VMEM
-    scratch = [
+    results = [
+        V((1, NW), F32), V((LAYERS, 3, CZ, CD), F32), V((CD, NL), F32), V((CD, TRACKS), F32),
+    ]
+    scratch = results + [
+        dma((LAYERS + 3,)),
         V((NS, T // NS, 128), jnp.int32), V((NS, T // NS, 128), jnp.int32), dma((NS,)), dma((NS,)),
         V((CD, TRACKS), BF16),
         V((CX, NL), BF16), V((CX, NW), BF16), V((LAYERS, 3, CX, C), BF16),
@@ -525,11 +542,9 @@
     hbm = pl.BlockSpec(memory_space=pl.ANY)
     score, conv_grad, stem_grad, head_grad = pl.pallas_call(
         tower,
-        out_shape=(
-            V((1, NW), F32), V((LAYERS, 3, CZ, CD), F32), V((CD, NL), F32), V((CD, TRACKS), F32),
-        ),
+        out_shape=tuple(results),
         in_specs=[vm, hbm, hbm, hbm, vm, vm, vm],
-        out_specs=(vm, vm, vm, vm),
+        out_specs=(hbm, hbm, hbm, hbm),
         scratch_shapes=scratch,
         compiler_params=pltpu.CompilerParams(
             collective_id=0, has_side_effects=True, vmem_limit_bytes=60 * 1024 * 1024

time: 138 us -> 138 us (level)
  no operation moved by 1% of the time
where the time goes in v4:
time: 138 us
  Pallas kernels  137 us (99%)
    pallas_call x1, Pallas kernels, shards(): pl.pallas_call(tower, out_shape=tuple(results), in_specs=[vm, hbm, hbm, h...  135 us

profile of v4, /device:TPU:1, one launch (start us, length us, event | category | flops | bytes accessed | tf_op | source)
XLA Modules:
  0.0 137.5 jit_solution(13481380117568955052)
XLA Ops:
  0.6 135.2 %shard_map.102 = (f32[1,512]{1,0:T(1,128)S(1)}, f32[5,3,24,96]{3,2,1,0:T(8,128)S(1)}, f32[96,512]{1,0:T(8,128)S(1)}, f32[96,5313]{1,0:T(8,128)S(1)}) custom-call(s32[256,128]{1,0:T(8,128)} %genome.1, bf16[96,512]{1,0:T(8,128)(2,1)} %stem.1, bf16[5,3,96,768]{3,2,1,0:T(8,128)(2,1)} %weight.1, bf16[96,5313]{1,0:T(8,128)(2,1)} %head.1, s32[1,512]{1,0:T(1,128)} %bitcast.5, ...), custom_call_target="tpu_custom_call" | custom-call | tf_op jit(solution)/shard_map/pallas_call | solution.py:543
  135.8 1.5 %shard_map.103 = (f32[1,512]{1,0:T(1,128)}, f32[5,3,24,96]{3,2,1,0:T(8,128)}, f32[96,512]{1,0:T(8,128)}, f32[96,5313]{1,0:T(8,128)}) custom-call(f32[1,512]{1,0:T(1,128)S(1)} %get-tuple-element.12.score, f32[5,3,24,96]{3,2,1,0:T(8,128)S(1)} %get-tuple-element.13.conv, f32[96,512]{1,0:T(8,128)S(1)} %get-tuple-element.14.stem, ...), custom_call_target="tpu_custom_call" | custom-call | tf_op jit(solution)/shard_map/pallas_call | solution.py:557

commit v5 on v3

--- a/solution.py
+++ b/solution.py
@@ -88,9 +88,14 @@
         pending.append(copy)
         return copy
 
-    def lead(copy):
-        pending[:] = [p for p in pending if p is not copy]
-        copy.wait_send()
+    def fire(copy):
+        copy.start()
+        return copy
+
+    def all_of(ref, sem):
+        pltpu.make_async_copy(ref, ref, sem).wait()
+
+    ending = []
 
     def x_at(j):
         return 2 * ((x + j) % NX) + q
@@ -113,7 +118,7 @@
             local.append(
                 pltpu.make_async_copy(
                     weight.at[l, k], wst.at[l, k + q * (2 - 2 * k), mine],
-                    local_sem.at[2 + 3 * l + k],
+                    local_sem.at[2 + l],
                 )
             )
     for copy in local:
@@ -139,18 +144,10 @@
 
     def gcopy(j):
         to = (s + j) % NS
-        return remote(gbuf.at[to], gen.at[s], gsend.at[j], grecv.at[j], to, c)
+        return remote(gbuf.at[to], gen.at[s], gsend.at[0], grecv.at[0], to, c)
 
     def gstart(j, _):
         gcopy(j).start()
-        return 0
-
-    def gwait(j, _):
-        gcopy(j).wait_recv()
-        return 0
-
-    def gdone(j, _):
-        gcopy(j).wait_send()
         return 0
 
     lax.fori_loop(1, NS, gstart, 0)
@@ -158,12 +155,13 @@
     pw = []
     for l in range(LAYERS):
         pw.append([
-            go(remote(
+            fire(remote(
                 weight.at[l, k], wst.at[l, k + (1 - q) * (2 - 2 * k), mine],
-                psend.at[2 + 3 * l + k], precv.at[2 + 3 * l + k], s, pc,
+                psend.at[2 + l], precv.at[2 + l], s, pc,
             ))
             for k in range(3)
         ])
+        ending.append((wst.at[l, :, mine], psend.at[2 + l]))
 
     gen[s] = gbuf[s]
     local[1].wait()
@@ -187,7 +185,7 @@
     target = 4 * (col % 128) + col // 128
     target = jnp.where(q == 0, target, NL - 1 - target)
     order = (row == target).astype(F32).astype(BF16)
-    lax.fori_loop(1, NS, gwait, 0)
+    all_of(gen.at[pl.ds(0, NS - 1)], grecv.at[0])
     bases = gen[...].reshape(T, 128)
     hot = jnp.concatenate([(bases == n).astype(F32).astype(BF16) for n in range(4)], axis=1)
     letters[...] = nt(hot, order).astype(BF16)
@@ -209,28 +207,24 @@
         act[l, x, 1] = a[CD:]
 
         def ring(slot, h, j, n):
-            return go(remote(
-                act.at[l, slot, h], act.at[l, slot, h], asend.at[l, n], arecv.at[l, n], s, x_at(j)
+            return fire(remote(
+                act.at[l, slot, h], act.at[l, slot, h], asend.at[l], arecv.at[l, min(n, 2)],
+                s, x_at(j),
             ))
 
         f0 = ring(x, 0, 1, 0)
         b1 = ring(x, 1, 3, 1)
         der[l] = half + (0.5 * ROOT) * state * (1.0 - th * th) * (1.0 + (3 * CUBE) * sq)
-        lead(f0)
-        f1 = ring(x, 1, 1, 2)
-        lead(b1)
-        b0 = ring(x, 0, 3, 3)
+        ring(x, 1, 1, 2)
+        ring(x, 0, 3, 3)
         f0.wait_recv()
-        fr = ring((x + 3) % NX, 0, 1, 4)
+        ring((x + 3) % NX, 0, 1, 4)
         b1.wait_recv()
-        br_ = ring((x + 1) % NX, 1, 3, 5)
-        for k in range(3):
-            local[2 + 3 * l + k].wait()
-            pw[l][k].wait_recv()
-        f1.wait_recv()
-        b0.wait_recv()
-        fr.wait_recv()
-        br_.wait_recv()
+        ring((x + 1) % NX, 1, 3, 5)
+        all_of(wst.at[l, :, mine], local_sem.at[2 + l])
+        all_of(wst.at[l, :, mine], precv.at[2 + l])
+        all_of(act.at[l, pl.ds(0, 2)], arecv.at[l, 2])
+        ending.append((act.at[l, pl.ds(0, 3)], asend.at[l]))
         p = jnp.dot(
             wst[l].reshape(3 * CX, C), act[l].reshape(C, T), preferred_element_type=F32
         )
@@ -248,53 +242,54 @@
 
     def one(j):
         to = (c + j) % NC
-        return remote(sone.at[c], sone.at[c], ssone.at[j], rsone.at[j], s, to)
-
-    ones = [go(one(j)) for j in range(1, NC)]
+        return remote(sone.at[c], sone.at[c], ssone.at[0], rsone.at[0], s, to)
+
+    for j in range(1, NC):
+        one(j).start()
+    ending.append((sone.at[pl.ds(0, NC - 1)], ssone.at[0]))
 
     def reduce_y(r, value):
         for i in range(2):
             for j in range(NY):
                 rys[r, i, j] = value[CD * i:CD * (i + 1), 128 * j:128 * (j + 1)].astype(BF16)
         return [
-            go(remote(
+            fire(remote(
                 rys.at[r, (q + i) % 2, (y + j) % NY], ryr.at[r, NY * i + j],
-                r_ys.at[r, NY * i + j], r_yr.at[r, NY * i + j], y_at(j), 2 * x + (q + i) % 2,
+                r_ys.at[r], r_yr.at[r], y_at(j), 2 * x + (q + i) % 2,
             ))
             for j in range(NY) for i in range(2) if i + j > 0
         ]
 
     def reduce_z(r, copies):
-        for copy in copies:
-            copy.wait_recv()
+        all_of(ryr.at[r, pl.ds(1, 2 * NY - 1)], r_yr.at[r])
+        ending.append((ryr.at[r, pl.ds(1, 2 * NY - 1)], r_ys.at[r]))
         total = rys[r, q, y].astype(F32)
         for i in range(1, 2 * NY):
             total = total + ryr[r, i].astype(F32)
         rzb[r, z] = total.astype(BF16)
         return [
-            go(remote(rzb.at[r, z], rzb.at[r, z], r_zs.at[r, j], r_zr.at[r, j], z_at(j), c))
+            fire(remote(rzb.at[r, z], rzb.at[r, z], r_zs.at[r], r_zr.at[r], z_at(j), c))
             for j in range(1, NZ)
         ]
 
     def reduce_g(r, copies):
-        for copy in copies:
-            copy.wait_recv()
+        all_of(rzb.at[r, pl.ds(1, NZ - 1)], r_zr.at[r])
+        ending.append((rzb.at[r, pl.ds(1, NZ - 1)], r_zs.at[r]))
         total = rzb[r, 0].astype(F32)
         for j in range(1, NZ):
             total = total + rzb[r, j].astype(F32)
         rgb[r, y] = total
         return [
-            go(remote(rgb.at[r, y], rgb.at[r, y], r_gs.at[r, j], r_gr.at[r, j], y_at(j), c))
+            fire(remote(rgb.at[r, y], rgb.at[r, y], r_gs.at[r], r_gr.at[r], y_at(j), c))
             for j in range(1, NY)
         ]
 
     def reduce_end(r, copies):
-        for copy in copies:
-            copy.wait_recv()
+        all_of(rgb.at[r, pl.ds(1, NY - 1)], r_gr.at[r])
+        ending.append((rgb.at[r, pl.ds(1, NY - 1)], r_gs.at[r]))
         return jnp.concatenate([rgb[r, j] for j in range(NY)], axis=1)
 
-    for copy in ones:
-        copy.wait_recv()
+    all_of(sone.at[pl.ds(0, NC - 1)], rsone.at[0])
     total = sone[0]
     for j in range(1, NC):
         total = total + sone[j]
@@ -302,24 +297,16 @@
 
     def two(j):
         to = (s + j) % NS
-        return remote(stwo.at[s], stwo.at[s], sstwo.at[j], rstwo.at[j], to, c)
+        return remote(stwo.at[s], stwo.at[s], sstwo.at[0], rstwo.at[0], to, c)
 
     def two_start(j, _):
         two(j).start()
         return 0
 
-    def two_wait(j, _):
-        two(j).wait_recv()
-        return 0
-
-    def two_done(j, _):
-        two(j).wait_send()
-        return 0
-
     lax.fori_loop(1, NS, two_start, 0)
     pool_copies = reduce_y(0, pooled)
     a2 = {4: share(4), 3: share(3)}
-    lax.fori_loop(1, NS, two_wait, 0)
+    all_of(stwo.at[pl.ds(0, NS - 1)], rstwo.at[0])
     score = stwo[0]
     for j in range(1, NS):
         score = score + stwo[j]
@@ -332,8 +319,8 @@
 
     def y_stage(item):
         l, copies = item
-        for copy in copies:
-            copy.wait_recv()
+        all_of(yrecv.at[l, pl.ds(1, NY - 1)], yr.at[l])
+        ending.append((yrecv.at[l, pl.ds(1, NY - 1)], ys.at[l]))
         own = pl.ds(pl.multiple_of(CX * y, CX), CX)
         total = wg[l, own].astype(F32)
         for j in range(1, NY):
@@ -342,8 +329,8 @@
         zacc[l] = total
         zsend[l] = total.astype(BF16)
         sends = [
-            go(remote(
-                zsend.at[l, (z + j) % NZ], zrecv.at[l, j], zs.at[l, j], zr.at[l, j], z_at(j), c
+            fire(remote(
+                zsend.at[l, (z + j) % NZ], zrecv.at[l, j], zs.at[l], zr.at[l], z_at(j), c
             ))
             for j in range(1, NZ)
         ]
@@ -351,8 +338,8 @@
 
     def z_stage(item):
         l, copies = item
-        for copy in copies:
-            copy.wait_recv()
+        all_of(zrecv.at[l, pl.ds(1, NZ - 1)], zr.at[l])
+        ending.append((zrecv.at[l, pl.ds(1, NZ - 1)], zs.at[l]))
         total = zacc[l, z]
         for j in range(1, NZ):
             total = total + zrecv[l, j].astype(F32)
@@ -387,7 +374,9 @@
                 bsend[l, i, h] = p[at:at + CD].astype(BF16)
 
         def shed(src, n, j):
-            return go(remote(src, brecv.at[l, n], bs.at[l, n], br.at[l, n], s, x_at(j)))
+            return fire(remote(
+                src, brecv.at[l, n], bs.at[l], br.at[l, min(n, 2)], s, x_at(j)
+            ))
 
         far = (x + 2) % NX
         right = (x + 1) % NX
@@ -403,10 +392,8 @@
             [jnp.where(first, vh, vl), v.astype(BF16), jnp.where(first, vl, vh)], axis=0
         )
         g = nt(act[l].reshape(C, T), own_taps)
-        lead(f1)
-        f0 = shed(bsend.at[l, right, 0], 2, 1)
-        lead(b0)
-        b1 = shed(bsend.at[l, left, 1], 3, 3)
+        shed(bsend.at[l, right, 0], 2, 1)
+        shed(bsend.at[l, left, 1], 3, 3)
         ucopy.wait_recv()
         a2[l].wait_recv()
         w = upx[l].astype(F32)
@@ -416,9 +403,9 @@
         )
         wg[l] = (g + nt(act2[l].reshape(C, T), far_taps)).astype(BF16)
         ysends = [
-            go(remote(
+            fire(remote(
                 wg.at[l, pl.ds(pl.multiple_of(CX * ((y + j) % NY), CX), CX)], yrecv.at[l, j],
-                ys.at[l, j], yr.at[l, j], y_at(j), c,
+                ys.at[l], yr.at[l], y_at(j), c,
             ))
             for j in range(1, NY)
         ]
@@ -426,10 +413,10 @@
         b0.wait_recv()
         at = pl.ds(pl.multiple_of(CX * right + CD, CD), CD)
         bcomb[l, 0] = (part[at] + brecv[l, 0].astype(F32)).astype(BF16)
-        fc = shed(bcomb.at[l, 0], 4, 1)
+        shed(bcomb.at[l, 0], 4, 1)
         at = pl.ds(pl.multiple_of(CX * left, CD), CD)
         bcomb[l, 1] = (part[at] + brecv[l, 1].astype(F32)).astype(BF16)
-        bc = shed(bcomb.at[l, 1], 5, 3)
+        shed(bcomb.at[l, 1], 5, 3)
         if waiting_y is not None:
             y_stage(waiting_y)
         waiting_y = (l, ysends)
@@ -449,10 +436,8 @@
         if l == LAYERS - 4:
             place(WHOLE // 2, WHOLE)
             head_out[:, WHOLE * CHUNK:] = spread_out(one_hot(WHOLE * CHUNK, REST))
-        f0.wait_recv()
-        b1.wait_recv()
-        fc.wait_recv()
-        bc.wait_recv()
+        all_of(brecv.at[l, pl.ds(2, 4)], br.at[l, 2])
+        ending.append((brecv.at[l], bs.at[l]))
         own0 = part[pl.ds(pl.multiple_of(CX * x, CD), CD)]
         own1 = part[pl.ds(pl.multiple_of(CX * x + CD, CD), CD)]
         low = own0 + brecv[l, 2].astype(F32) + brecv[l, 5].astype(F32)
@@ -470,8 +455,10 @@
     stem_copies = reduce_g(1, stem_copies)
     stem_out[...] = reduce_end(1, stem_copies)
 
-    lax.fori_loop(1, NS, gdone, 0)
-    lax.fori_loop(1, NS, two_done, 0)
+    all_of(gen.at[pl.ds(0, NS - 1)], gsend.at[0])
+    all_of(stwo.at[pl.ds(0, NS - 1)], sstwo.at[0])
+    for ref, sem in ending:
+        all_of(ref, sem)
     for copy in pending:
         copy.wait_send()
 
@@ -499,27 +486,26 @@
     dma = pltpu.SemaphoreType.DMA
     V = pltpu.VMEM
     scratch = [
-        V((NS, T // NS, 128), jnp.int32), V((NS, T // NS, 128), jnp.int32), dma((NS,)), dma((NS,)),
+        V((NS, T // NS, 128), jnp.int32), V((NS, T // NS, 128), jnp.int32), dma((1,)), dma((1,)),
         V((CD, TRACKS), BF16),
         V((CX, NL), BF16), V((CX, NW), BF16), V((LAYERS, 3, CX, C), BF16),
-        dma((17,)), dma((17,)), dma((17,)),
+        dma((2 + LAYERS,)), dma((2 + LAYERS,)), dma((2 + LAYERS,)),
         V((T, NL), BF16),
         V((LAYERS, NX, 2, CD, T), BF16), V((LAYERS, NX, 2, CD, T), BF16),
-        V((LAYERS, CX, T), F32), dma((LAYERS, 6)), dma((LAYERS, 6)),
+        V((LAYERS, CX, T), F32), dma((LAYERS,)), dma((LAYERS, 3)),
         dma((LAYERS,)), dma((LAYERS,)),
-        V((NC, 1, NW), F32), dma((NC,)), dma((NC,)),
-        V((NS, 1, NW), F32), dma((NS,)), dma((NS,)),
+        V((NC, 1, NW), F32), dma((1,)), dma((1,)),
+        V((NS, 1, NW), F32), dma((1,)), dma((1,)),
         V((C, T), F32), V((LAYERS, NX, 2, CD, T), BF16), V((LAYERS, 6, CD, T), BF16),
-        V((LAYERS, 2, CD, T), BF16), dma((LAYERS, 6)), dma((LAYERS, 6)),
+        V((LAYERS, 2, CD, T), BF16), dma((LAYERS,)), dma((LAYERS, 3)),
         V((LAYERS, CX, T), BF16), V((LAYERS, CD, T), BF16), dma((LAYERS,)), dma((LAYERS,)),
         V((LAYERS, C, KO), BF16), V((LAYERS, NY, CX, KO), BF16),
-        dma((LAYERS, NY)), dma((LAYERS, NY)),
+        dma((LAYERS,)), dma((LAYERS,)),
         V((LAYERS, NZ, CZ, KO), F32), V((LAYERS, NZ, CZ, KO), BF16),
-        V((LAYERS, NZ, CZ, KO), BF16), dma((LAYERS, NZ)), dma((LAYERS, NZ)),
+        V((LAYERS, NZ, CZ, KO), BF16), dma((LAYERS,)), dma((LAYERS,)),
         V((2, 2, NY, CD, 128), BF16), V((2, 2 * NY, CD, 128), BF16),
         V((2, NZ, CD, 128), BF16), V((2, NY, CD, 128), F32),
-        dma((2, 2 * NY)), dma((2, 2 * NY)), dma((2, NZ)), dma((2, NZ)),
-        dma((2, NY)), dma((2, NY)), V((KO, NW), BF16),
+        dma((2,)), dma((2,)), dma((2,)), dma((2,)), dma((2,)), dma((2,)), V((KO, NW), BF16),
     ]
     vm = pl.BlockSpec(memory_space=pltpu.VMEM)
     hbm = pl.BlockSpec(memory_space=pl.ANY)

time: 138 us -> 135 us (0.978)
  Pallas kernels: 136 us -> 134 us
    pallas_call x1, Pallas kernels: 135 us -> 132 us  [shards(): pl.pallas_call(tower, out_shape=(V((1, NW), F32), V((LAYERS, 3, CZ, CD),...]
where the time goes in v5:
time: 135 us; the launch traced here: 134 us
  Pallas kernels  134 us (99%)
    pallas_call x1, Pallas kernels, shards(): pl.pallas_call(tower, out_shape=(V((1, NW), F32), V((LAYERS, 3, CZ, CD),...  132 us

profile of v5, /device:TPU:1, one launch (start us, length us, event | category | flops | bytes accessed | tf_op | source)
XLA Modules:
  0.0 134.5 jit_solution(4630678739486630767)
XLA Ops:
  0.6 132.1 %shard_map.102 = (f32[1,512]{1,0:T(1,128)S(1)}, f32[5,3,24,96]{3,2,1,0:T(8,128)S(1)}, f32[96,512]{1,0:T(8,128)S(1)}, f32[96,5313]{1,0:T(8,128)S(1)}) custom-call(s32[256,128]{1,0:T(8,128)} %genome.1, bf16[96,512]{1,0:T(8,128)(2,1)} %stem.1, bf16[5,3,96,768]{3,2,1,0:T(8,128)(2,1)} %weight.1, bf16[96,5313]{1,0:T(8,128)(2,1)} %head.1, s32[1,512]{1,0:T(1,128)} %bitcast.5, ...), custom_call_target="tpu_custom_call" | custom-call | tf_op jit(solution)/shard_map/pallas_call | solution.py:512
  132.8 1.5 %shard_map.103 = (f32[1,512]{1,0:T(1,128)}, f32[5,3,24,96]{3,2,1,0:T(8,128)}, f32[96,512]{1,0:T(8,128)}, f32[96,5313]{1,0:T(8,128)}) custom-call(f32[1,512]{1,0:T(1,128)S(1)} %get-tuple-element.12.score, f32[5,3,24,96]{3,2,1,0:T(8,128)S(1)} %get-tuple-element.13.conv, f32[96,512]{1,0:T(8,128)S(1)} %get-tuple-element.14.stem, ...), custom_call_target="tpu_custom_call" | custom-call | tf_op jit(solution)/shard_map/pallas_call | solution.py:528

commit v6 on v5

--- a/solution.py
+++ b/solution.py
@@ -447,12 +447,12 @@
     stem_copies = reduce_y(
         1, jnp.dot(grad.astype(BF16), letters[...], preferred_element_type=F32)
     )
+    stem_copies = reduce_z(1, stem_copies)
     y_stage(waiting_y)
     z_stage(waiting_z.pop(0))
-    stem_copies = reduce_z(1, stem_copies)
+    stem_copies = reduce_g(1, stem_copies)
     while waiting_z:
         z_stage(waiting_z.pop(0))
-    stem_copies = reduce_g(1, stem_copies)
     stem_out[...] = reduce_end(1, stem_copies)
 
     all_of(gen.at[pl.ds(0, NS - 1)], gsend.at[0])

time: 135 us -> 134 us (level)
  no operation moved by 1% of the time
where the time goes in v6:
time: 134 us
  Pallas kernels  133 us (99%)
    pallas_call x1, Pallas kernels, shards(): pl.pallas_call(tower, out_shape=(V((1, NW), F32), V((LAYERS, 3, CZ, CD),...  132 us

profile of v6, /device:TPU:1, one launch (start us, length us, event | category | flops | bytes accessed | tf_op | source)
XLA Modules:
  0.0 134.2 jit_solution(6991923383222117086)
XLA Ops:
  0.6 131.9 %shard_map.102 = (f32[1,512]{1,0:T(1,128)S(1)}, f32[5,3,24,96]{3,2,1,0:T(8,128)S(1)}, f32[96,512]{1,0:T(8,128)S(1)}, f32[96,5313]{1,0:T(8,128)S(1)}) custom-call(s32[256,128]{1,0:T(8,128)} %genome.1, bf16[96,512]{1,0:T(8,128)(2,1)} %stem.1, bf16[5,3,96,768]{3,2,1,0:T(8,128)(2,1)} %weight.1, bf16[96,5313]{1,0:T(8,128)(2,1)} %head.1, s32[1,512]{1,0:T(1,128)} %bitcast.5, ...), custom_call_target="tpu_custom_call" | custom-call | tf_op jit(solution)/shard_map/pallas_call | solution.py:512
  132.5 1.5 %shard_map.103 = (f32[1,512]{1,0:T(1,128)}, f32[5,3,24,96]{3,2,1,0:T(8,128)}, f32[96,512]{1,0:T(8,128)}, f32[96,5313]{1,0:T(8,128)}) custom-call(f32[1,512]{1,0:T(1,128)S(1)} %get-tuple-element.12.score, f32[5,3,24,96]{3,2,1,0:T(8,128)S(1)} %get-tuple-element.13.conv, f32[96,512]{1,0:T(8,128)S(1)} %get-tuple-element.14.stem, ...), custom_call_target="tpu_custom_call" | custom-call | tf_op jit(solution)/shard_map/pallas_call | solution.py:528
